TPU v7x, 128 devices: a whole 4x4x4 slice. The times are simulated.
128 devices in a mesh: grp: 16 (over y, z_lo, core), tile: 8 (over z_hi, x).
Axes of the slice: x: 4, y: 4, z: 4 (z_hi: 2, z_lo: 2; z = z_hi * 2 + z_lo), core: 2. Of those that a mesh axis runs over, the one named last changes fastest.
Arguments:
- parent_so2: float32 [4, 1024, 1024], P(None, 'grp', 'tile'), may hold values from 0.1 to 10
- wind_east: float32 [4, 1024, 1024], P(None, 'grp', 'tile'), may hold values from -0.2 to 0.2
- wind_north: float32 [4, 1024, 1024], P(None, 'grp', 'tile'), may hold values from -0.2 to 0.2
- diffusivity: float32 [4, 1024, 1024], P(None, 'grp', 'tile'), may hold values from 0.01 to 0.25
- nest_so2: float32 [16, 4, 320, 320], P('grp', None, 'tile'), may hold values from 0.1 to 10
- nest_rows: int32 [16], replicated, may hold values from 0 to 15, as said below
- nest_offset: int32 [16], replicated, may hold values from 1 to 31
- nest_left: int32 [16], replicated, may hold values from 1 to 991
- nest_height: int32 [16], replicated, may hold values from 16 to 32
- nest_width: int32 [16], replicated, may hold values from 16 to 32
Outputs:
- parent_next: float32 [4, 1024, 1024], P(None, 'grp', 'tile')
- nest_next: float32 [16, 4, 320, 320], P('grp', None, 'tile')
Inputs may be any that keep to these rules, and one draw needn't show every extreme that they name: `nest_rows`: each of 0 to 15 appears once.
All inputs are finite; a program needn't handle non-finite values.
Results may differ from a plain program's by a relative error of at most 0.0001.
Values sent between devices are 32-bit elements; how exact they have to be, the bound alone decides.
No kernel may reach another device: no remote copies, remote signals or barrier semaphores. Data moves between devices by JAX's collectives and lax.ppermute only.
A program may use at most 64 MiB of HBM per device.

v0:
```python
import functools
import jax
import jax.numpy as jnp
from jax import lax
from jax.experimental import pallas as pl
from jax.experimental.pallas import tpu as pltpu
from jax.sharding import PartitionSpec as P

RATIO = 10
FR = 32
LEV = 4
ROWS = 64
COLS = 128
OWN = 40
WIDE = 320
GROUPS = 16
TILES = 8
SPAN = FR + 2
WIN = 40
HALO = 120
MIX = 0.02

SMEM = pl.BlockSpec(memory_space=pltpu.SMEM)
ANY = pl.BlockSpec(memory_space=pl.ANY)
VMEM = pl.BlockSpec(memory_space=pltpu.VMEM)


def width_of(chunk):
    return min(128, WIDE - 128 * chunk)


def nest_over(rows, group):
    found = jnp.int32(0)
    for i in range(GROUPS):
        found = jnp.where(rows[i] == group, jnp.int32(i), found)
    return found


def lanes(shape):
    return lax.broadcasted_iota(jnp.int32, shape, 1)


def pack_kernel(rows, offs, left, so2, east, north, diff, nest, send, edges, x, nx, sems):
    t = lax.axis_index("tile")
    g = lax.axis_index("grp")
    loads = [
        pltpu.make_async_copy(f, x.at[pl.ds(4 * i, 4), pl.ds(0, ROWS), :], sems.at[i])
        for i, f in enumerate((so2, east, north, diff))
    ]
    loads.append(pltpu.make_async_copy(nest.at[0], nx, sems.at[4]))
    for c in loads:
        c.start()
    n = nest_over(rows, g)
    top = offs[n] - 1
    base = 128 * t + 1 - left[n] + 1024
    x[:, ROWS : ROWS + 8, :] = jnp.zeros((16, 8, 128), jnp.float32)
    lane = lanes((8, 128))
    before = jnp.where(t > 0, t - 1, t + 2)
    after = jnp.where(t < TILES - 1, t + 1, t - 2)
    loads[4].wait()
    for l in range(LEV):
        for m in range(3):
            w = width_of(m)
            at = 10 * (3 * l + m)
            rows_at = pl.ds(WIN + 8 + at, 10)
            send[before, rows_at, 0:w] = nx[l, 0:10, 128 * m : 128 * m + w]
            send[after, rows_at, 0:w] = nx[l, OWN - 10 : OWN, 128 * m : 128 * m + w]
    for c in loads[:4]:
        c.wait()
    for l in range(LEV):
        edges[l : l + 1, :] = x[l, 0:1, :]
        edges[4 + l : 5 + l, :] = x[4 + l, 0:1, :]
        edges[8 + l : 9 + l, :] = x[l, ROWS - 1 : ROWS, :]
        edges[12 + l : 13 + l, :] = x[4 + l, ROWS - 1 : ROWS, :]
    first = jnp.zeros((8, 128), jnp.float32)
    last = jnp.zeros((8, 128), jnp.float32)
    for p in range(8):
        plane = p if p < 4 else p + 4
        for b in range(8):
            k = 8 * p + b
            v = x[plane, 8 * b : 8 * b + 8, :]
            first = jnp.where(lane == k, pltpu.roll(v, k, 1), first)
            last = jnp.where(lane == k, pltpu.roll(v, k + 1, 1), last)
    shifts = [lax.rem(base + SPAN * f, 128) for f in range(3)]
    kshifts = [lax.rem(base + 32 * l - 1, 128) for l in range(LEV)]
    for d in range(TILES):
        for l in range(LEV):
            part = [
                pltpu.roll(x[4 * f + l, pl.ds(top + 4 * d, 8), :], shifts[f], 1) for f in range(3)
            ]
            send[d, 8 * l : 8 * l + 8, :] = jnp.where(
                lane < SPAN, part[0], jnp.where(lane < 2 * SPAN, part[1], part[2])
            )
        part = [pltpu.roll(x[12 + l, pl.ds(top + 4 * d, 8), :], kshifts[l], 1) for l in range(LEV)]
        send[d, 32:40, :] = jnp.where(
            lane < 64,
            jnp.where(lane < 32, part[0], part[1]),
            jnp.where(lane < 96, part[2], part[3]),
        )
        send[d, 40:48, :] = jnp.where(d < t, first, last)


def merge_kernel(rows, left, got, edges, send):
    g = lax.axis_index("grp")
    n = nest_over(rows, g)
    start = left[n] - 1
    first = lax.div(start, COLS)
    second = jnp.minimum(first + 1, TILES - 1)
    send[jnp.where(g > 0, g - 1, g + 2), WIN : WIN + 8, :] = edges[0:8, :]
    send[jnp.where(g < GROUPS - 1, g + 1, g - 2), WIN : WIN + 8, :] = edges[8:16, :]
    room = COLS - (start - COLS * first)
    lane = lanes((8, 128))
    col = lane - jnp.where(lane >= SPAN, SPAN, 0) - jnp.where(lane >= 2 * SPAN, SPAN, 0)
    kcol = (lane & 31) + 1
    for l in range(5):
        q = slice(8 * l, 8 * l + 8)
        here = (col if l < 4 else kcol) < room
        send[n, q, :] = jnp.where(here, got[first, q, :], got[second, q, :])


def from_left(chunks, lane):
    turned = [pltpu.roll(c, 1, 1) for c in chunks]
    return [jnp.where(lane == 0, turned[m - 1], turned[m]) for m in range(3)]


def from_right(chunks, lane):
    turned = [pltpu.roll(c, 127, 1) for c in chunks]
    return [jnp.where(lane == 127, turned[(m + 1) % 3], turned[m]) for m in range(3)]


def pos(v):
    return jnp.maximum(v, 0.0)


def neg(v):
    return jnp.minimum(v, 0.0)


def fine_kernel(
    rows, left, height, width, got_tile, got_grp, nest,
    fine_out, back,
    nx, e, c, u, v, kz, raw, am, ap, bm, bp, ac, sums, sems,
):
    t = lax.axis_index("tile")
    g = lax.axis_index("grp")
    src = rows[g]
    prev_t = jnp.maximum(t - 1, 0)
    next_t = jnp.minimum(t + 1, TILES - 1)
    load = pltpu.make_async_copy(nest.at[0], nx, sems.at[0])
    load.start()
    lane = lanes((8, 128))
    sub = lax.broadcasted_iota(jnp.int32, (8, 128), 0)
    zero = jnp.zeros((8, 128), jnp.float32)
    for p in range(2):
        for l in range(LEV):
            for m in range(3):
                c[p, l, m, 0:8, :] = zero
                c[p, l, m, 72:80, :] = zero
    for m in range(3):
        fine_col = 128 * m + lane
        under = (fine_col * 6554) >> 16
        pick = jnp.where(fine_col < WIDE, under + 1, jnp.where(fine_col == WIDE, SPAN - 1, 0))
        kpick = jnp.minimum(under, FR - 1)
        for l in range(LEV):
            block = got_grp[src, 8 * l : 8 * l + 8, :]
            for f in range(3):
                e[4 * f + l, m] = jnp.take_along_axis(block, pick + SPAN * f, axis=1)
            e[12 + l, m] = jnp.take_along_axis(got_grp[src, 32:40, :], kpick + 32 * l, axis=1)
    load.wait()
    for l in range(LEV):
        for m in range(3):
            n = width_of(m)
            at = 10 * (3 * l + m)
            raw[l, m, 8:18, :] = got_tile[prev_t, pl.ds(WIN + 8 + at, 10), :]
            raw[l, m, 18:58, 0:n] = nx[l, :, 128 * m : 128 * m + n]
            raw[l, m, 58:68, :] = got_tile[next_t, pl.ds(WIN + 8 + at, 10), :]
    last_row = RATIO * height[g]
    last_col = RATIO * width[g]
    first_row = OWN * t - 10

    def spread(p, m, i):
        lo, hi = (8 * i) // 10, min((8 * i + 7) // 10, 5)
        low = jnp.broadcast_to(e[p, m, lo : lo + 1, :], (8, 128))
        if lo == hi:
            return low
        high = jnp.broadcast_to(e[p, m, hi : hi + 1, :], (8, 128))
        return jnp.where(sub < 10 * hi - 8 * i, low, high)

    for i in range(8):
        r = 8 + 8 * i
        row = first_row + 8 * i + sub
        row_in = (row >= 0) & (row < last_row)
        for m in range(3):
            active = row_in & (128 * m + lane < last_col)
            for l in range(LEV):
                c[0, l, m, r : r + 8, :] = jnp.where(active, raw[l, m, r : r + 8, :], spread(l, m, i))
                u[l, m, r : r + 8, :] = spread(4 + l, m, i)
                v[l, m, r : r + 8, :] = spread(8 + l, m, i)
    for i in range(8):
        r = 8 + 8 * i
        local = 8 * i + sub
        row = first_row + local
        row_in = (row >= 0) & (row < last_row) & (local >= 1) & (local <= 58)
        inside = [row_in & (128 * m + lane < last_col) for m in range(3)]
        faces = []
        for m in range(3):
            ks = [spread(12 + l, m, i) for l in range(LEV)]
            faces.append([(0.05 * (ks[l] + ks[l + 1])) for l in range(LEV - 1)])
            for l in range(LEV - 1):
                kz[l, m, 8 * i : 8 * i + 8, :] = jnp.where(inside[m], faces[m][l], 0.0)
        for l in range(LEV):
            vs = [v[l, m, r : r + 8, :] for m in range(3)]
            before = from_left(vs, lane)
            after = from_right(vs, lane)
            for m in range(3):
                here = u[l, m, r : r + 8, :]
                u_lo = 0.5 * (u[l, m, r - 1 : r + 7, :] + here)
                u_hi = 0.5 * (here + u[l, m, r + 1 : r + 9, :])
                v_lo = 0.5 * (before[m] + vs[m])
                v_hi = 0.5 * (vs[m] + after[m])
                mid = (1.0 - 4.0 * MIX) - pos(u_hi) + neg(u_lo) - pos(v_hi) + neg(v_lo)
                if l > 0:
                    mid = mid - faces[m][l - 1]
                if l < LEV - 1:
                    mid = mid - faces[m][l]
                q = slice(8 * i, 8 * i + 8)
                ac[l, m, q, :] = jnp.where(inside[m], mid, 1.0)
                am[l, m, q, :] = jnp.where(inside[m], MIX + pos(u_lo), 0.0)
                ap[l, m, q, :] = jnp.where(inside[m], MIX - neg(u_hi), 0.0)
                bm[l, m, q, :] = jnp.where(inside[m], MIX + pos(v_lo), 0.0)
                bp[l, m, q, :] = jnp.where(inside[m], MIX - neg(v_hi), 0.0)

    def advance(old, new):
        for i in range(8):
            r = 8 + 8 * i
            q = slice(8 * i, 8 * i + 8)
            now = [[c[old, l, m, r : r + 8, :] for m in range(3)] for l in range(LEV)]
            flow = [[kz[l, m, q, :] for m in range(3)] for l in range(LEV - 1)]
            for l in range(LEV):
                before = from_left(now[l], lane)
                after = from_right(now[l], lane)
                for m in range(3):
                    value = ac[l, m, q, :] * now[l][m]
                    value = value + am[l, m, q, :] * c[old, l, m, r - 1 : r + 7, :]
                    value = value + ap[l, m, q, :] * c[old, l, m, r + 1 : r + 9, :]
                    value = value + bm[l, m, q, :] * before[m]
                    value = value + bp[l, m, q, :] * after[m]
                    if l > 0:
                        value = value + flow[l - 1][m] * now[l - 1][m]
                    if l < LEV - 1:
                        value = value + flow[l][m] * now[l + 1][m]
                    c[new, l, m, r : r + 8, :] = value

    def pair(_, carry):
        advance(0, 1)
        advance(1, 0)
        return carry

    lax.fori_loop(0, RATIO // 2, pair, 0)
    for l in range(LEV):
        for m in range(3):
            n = width_of(m)
            fine_out[0, l, :, 128 * m : 128 * m + n] = c[0, l, m, 18:58, 0:n]
            for a in range(4):
                band = c[0, l, m, 18 + 10 * a : 28 + 10 * a, :]
                sums[m, 4 * l + a : 4 * l + a + 1, :] = jnp.sum(band, axis=0, keepdims=True)
    mean = jnp.zeros((16, 128), jnp.float32)
    for m in range(3):
        k = 128 * m + lax.broadcasted_iota(jnp.int32, (128, 128), 0)
        chosen = ((k * 6554) >> 16) == lanes((128, 128))
        pick = jnp.where(chosen & (k < WIDE), 1.0, 0.0)
        mean = mean + jnp.dot(
            sums[m], pick, precision=lax.Precision.HIGHEST, preferred_element_type=jnp.float32
        )
    mean = mean * (1.0 / (RATIO * RATIO))
    lane4 = lanes((4, 128))
    value = jnp.zeros((4, 128), jnp.float32)
    turned = [mean if l == 0 else pltpu.roll(mean, 32 * l, 1) for l in range(LEV)]
    for l in range(LEV):
        inside = (lane4 >= 32 * l) & (lane4 < 32 * l + 32)
        value = jnp.where(inside, turned[l][4 * l : 4 * l + 4, :], value)
    tile_a = lax.div(left[g], COLS)
    tile_b = jnp.where(tile_a < TILES - 1, tile_a + 1, tile_a - 1)
    back[TILES * src + tile_a] = value
    back[TILES * src + tile_b] = value


def step_kernel(got_tile, got_grp, so2, east, north, diff, stepped, px, vk, sems):
    t = lax.axis_index("tile")
    g = lax.axis_index("grp")
    prev_t = jnp.maximum(t - 1, 0)
    next_t = jnp.minimum(t + 1, TILES - 1)
    prev_g = jnp.maximum(g - 1, 0)
    next_g = jnp.minimum(g + 1, GROUPS - 1)
    copies = [
        (so2, px.at[pl.ds(0, 4), pl.ds(8, ROWS), :]),
        (east, px.at[pl.ds(4, 4), pl.ds(8, ROWS), :]),
        (north, vk.at[pl.ds(0, 4)]),
        (diff, vk.at[pl.ds(4, 4)]),
    ]
    copies = [pltpu.make_async_copy(s, d, sems.at[i]) for i, (s, d) in enumerate(copies)]
    for copy in copies:
        copy.start()
    lane = lanes((8, 128))
    for copy in copies:
        copy.wait()
    for p in range(8):
        px[p, 7:8, :] = jnp.where(g > 0, got_grp[prev_g, WIN + p : WIN + p + 1, :], 0.0)
        px[p, 72:73, :] = jnp.where(g < GROUPS - 1, got_grp[next_g, WIN + p : WIN + p + 1, :], 0.0)
    edge_l = jnp.where(t > 0, got_tile[prev_t, WIN : WIN + 8, :], 0.0)
    edge_r = jnp.where(t < TILES - 1, got_tile[next_t, WIN : WIN + 8, :], 0.0)
    for b in range(8):
        r = 8 + 8 * b
        q = slice(8 * b, 8 * b + 8)
        now = [px[l, r : r + 8, :] for l in range(LEV)]
        ks = [vk[4 + l, q, :] for l in range(LEV)]
        between = [0.5 * (ks[l] + ks[l + 1]) * (now[l + 1] - now[l]) for l in range(LEV - 1)]
        for l in range(LEV):
            here = now[l]
            k, kv = 8 * l + b, 32 + 8 * l + b
            wind = vk[l, q, :]
            c_w = jnp.where(lane == 0, pltpu.roll(edge_l, (128 - k) % 128, 1), pltpu.roll(here, 1, 1))
            c_e = jnp.where(lane == 127, pltpu.roll(edge_r, 127 - k, 1), pltpu.roll(here, 127, 1))
            v_w = jnp.where(lane == 0, pltpu.roll(edge_l, 128 - kv, 1), pltpu.roll(wind, 1, 1))
            v_e = jnp.where(lane == 127, pltpu.roll(edge_r, 127 - kv, 1), pltpu.roll(wind, 127, 1))
            c_n = px[l, r - 1 : r + 7, :]
            c_s = px[l, r + 1 : r + 9, :]
            flow = px[4 + l, r : r + 8, :]
            u_lo = 0.5 * (px[4 + l, r - 1 : r + 7, :] + flow)
            u_hi = 0.5 * (flow + px[4 + l, r + 1 : r + 9, :])
            v_lo = 0.5 * (v_w + wind)
            v_hi = 0.5 * (wind + v_e)
            value = (
                here
                - ((pos(u_hi) * here + neg(u_hi) * c_s) - (pos(u_lo) * c_n + neg(u_lo) * here))
                - ((pos(v_hi) * here + neg(v_hi) * c_e) - (pos(v_lo) * c_w + neg(v_lo) * here))
                + MIX * (c_n + c_s + c_w + c_e - 4.0 * here)
            )
            if l < LEV - 1:
                value = value + between[l]
            if l > 0:
                value = value - between[l - 1]
            stepped[l, q, :] = value


def place_kernel(rows, offs, left, height, width, stepped, got, out, s, sems):
    t = lax.axis_index("tile")
    g = lax.axis_index("grp")
    n = nest_over(rows, g)
    lf = left[n]
    wd = width[n]

    @pl.when((lf < COLS * t + COLS) & (lf + wd > COLS * t))
    def _():
        off = offs[n]
        base = pl.multiple_of(lax.div(off, 8) * 8, 8)
        load_s = pltpu.make_async_copy(stepped.at[:, pl.ds(base, 40), :], s, sems.at[0])
        load_s.start()
        lane = lanes((FR, 128)) + COLS * t
        row = lax.broadcasted_iota(jnp.int32, (FR, 128), 0)
        covered = (lane >= lf) & (lane < lf + wd) & (row < height[n])
        load_s.wait()
        for l in range(LEV):
            turned = pltpu.roll(got[n], lax.rem(lf - COLS * t - 32 * l + 2048, 128), 1)
            at = pl.ds(off - base, FR)
            s[l, at, :] = jnp.where(covered, turned, s[l, at, :])
        store = pltpu.make_async_copy(s, out.at[:, pl.ds(base, 40), :], sems.at[1])
        store.start()
        store.wait()


def shards(so2, east, north, diff, nest, rows, offs, left, height, width):
    f32 = jnp.float32
    shape = jax.ShapeDtypeStruct
    dma = pltpu.SemaphoreType.DMA
    field = functools.partial(pltpu.VMEM, dtype=f32)
    near = functools.partial(pltpu.with_memory_space_constraint, memory_space=pltpu.VMEM)
    send, edges = pl.pallas_call(
        pack_kernel,
        out_shape=(field((TILES, WIN + 8 + HALO, 128)), field((16, 128))),
        in_specs=[SMEM] * 3 + [ANY] * 5,
        out_specs=(VMEM, VMEM),
        scratch_shapes=[field((16, ROWS + 8, 128)), field((LEV, OWN, WIDE)), dma((5,))],
        name="pack",
    )(rows, offs, left, so2, east, north, diff, nest)
    got_tile = near(lax.all_to_all(send, "tile", 0, 0))
    send = pl.pallas_call(
        merge_kernel,
        out_shape=field((GROUPS, WIN + 8, 128)),
        in_specs=[SMEM] * 2 + [VMEM, VMEM],
        out_specs=VMEM,
        name="merge",
    )(rows, left, got_tile, near(edges))
    got_grp = near(lax.all_to_all(send, "grp", 0, 0))
    nest_next, back = pl.pallas_call(
        fine_kernel,
        out_shape=(
            shape((1, LEV, OWN, WIDE), f32),
            field((GROUPS * TILES, 4, 128)),
        ),
        in_specs=[SMEM] * 4 + [VMEM] * 2 + [ANY],
        out_specs=(VMEM, VMEM),
        scratch_shapes=[
            field((LEV, OWN, WIDE)),
            field((16, 3, 8, 128)),
            field((2, LEV, 3, 80, 128)),
            field((LEV, 3, 80, 128)),
            field((LEV, 3, 80, 128)),
            field((LEV - 1, 3, 64, 128)),
            field((LEV, 3, 80, 128)),
            field((LEV, 3, 64, 128)),
            field((LEV, 3, 64, 128)),
            field((LEV, 3, 64, 128)),
            field((LEV, 3, 64, 128)),
            field((LEV, 3, 64, 128)),
            field((3, 16, 128)),
            dma((1,)),
        ],
        name="fine",
    )(rows, left, height, width, got_tile, got_grp, nest)
    stepped = pl.pallas_call(
        step_kernel,
        out_shape=shape((LEV, ROWS, COLS), f32),
        in_specs=[VMEM] * 2 + [ANY] * 4,
        out_specs=VMEM,
        scratch_shapes=[field((8, ROWS + 16, 128)), field((8, ROWS, 128)), dma((4,))],
        name="step",
    )(got_tile, got_grp, so2, east, north, diff)
    got = lax.all_to_all(back, ("grp", "tile"), 0, 0)
    got = near(got.reshape(GROUPS, FR, 128))
    parent_next = pl.pallas_call(
        place_kernel,
        out_shape=shape((LEV, ROWS, COLS), f32),
        in_specs=[SMEM] * 5 + [ANY, VMEM],
        out_specs=ANY,
        scratch_shapes=[field((LEV, 40, 128)), dma((2,))],
        input_output_aliases={5: 0},
        name="place",
    )(rows, offs, left, height, width, stepped, got)
    return parent_next, nest_next


def solution(mesh):
    in_specs = (
        P(None, "grp", "tile"),
        P(None, "grp", "tile"),
        P(None, "grp", "tile"),
        P(None, "grp", "tile"),
        P("grp", None, "tile", None),
        P(),
        P(),
        P(),
        P(),
        P(),
    )
    out_specs = (P(None, "grp", "tile"), P("grp", None, "tile", None))
    return jax.shard_map(shards, mesh=mesh, in_specs=in_specs, out_specs=out_specs, check_vma=False)
```

profile of v0, /device:TPU:1, one launch (start us, length us, event | category | flops | bytes accessed | tf_op | source)
XLA Modules:
  0.0 61.9 jit_solution(3541324350876435262)
XLA Ops:
  0.6 2.3 %pack.1 = (f32[8,168,128]{2,1,0:T(8,128)S(1)}, f32[16,128]{1,0:T(8,128)S(1)}) custom-call(s32[16]{0:T(128)} %rows.7, s32[16]{0:T(128)} %offs.3, s32[16]{0:T(128)} %left.7, f32[4,64,128]{2,1,0:T(8,128)} %so2.3, f32[4,64,128]{2,1,0:T(8,128)} %east.3, f32[4,64,128]{2,1,0:T(8,128)} %north.3, f32[4,64,128]{2,1,0:T(8,128)} %diff.3, f32[1,4,40,320]{3,2,1,0:T(8,128)} %nest.3), custom_call_target="tpu_custom_call" | custom-call | tf_op jit(solution)/shard_map/pack/pallas_call | solution.py:378
  2.9 20.7 %all_to_all.15.got.got_tile = f32[8,168,128]{2,1,0:T(8,128)S(1)} all-to-all(f32[8,168,128]{2,1,0:T(8,128)S(1)} %get-tuple-element.6), channel_id=1, replica_groups=mesh['grp'=16,'tile'=8] {'tile'}, dimensions={0} | all-to-all | bytes 1376256 | tf_op jit(solution)/shard_map/all_to_all | solution.py:386
  23.6 0.7 %merge.1 = f32[16,48,128]{2,1,0:T(8,128)S(1)} custom-call(s32[16]{0:T(128)} %rows.7, s32[16]{0:T(128)} %left.7, f32[8,168,128]{2,1,0:T(8,128)S(1)} %all_to_all.15.got.got_tile, f32[16,128]{1,0:T(8,128)S(1)} %get-tuple-element.7.edges), custom_call_target="tpu_custom_call" | custom-call | tf_op jit(solution)/shard_map/merge/pallas_call | solution.py:387
  24.3 14.9 %all_to_all.16.got_grp = f32[16,48,128]{2,1,0:T(8,128)S(1)} all-to-all(f32[16,48,128]{2,1,0:T(8,128)S(1)} %merge.1), channel_id=1, replica_groups=mesh['grp'=16,'tile'=8] {'grp'}, dimensions={0} | all-to-all | bytes 786432 | tf_op jit(solution)/shard_map/all_to_all | solution.py:394
  39.2 6.4 %fine.1 = (f32[1,4,40,320]{3,2,1,0:T(8,128)}, f32[128,4,128]{2,1,0:T(4,128)}) custom-call(s32[16]{0:T(128)} %rows.7, s32[16]{0:T(128)} %left.7, s32[16]{0:T(128)} %height.3, s32[16]{0:T(128)} %width.3, f32[8,168,128]{2,1,0:T(8,128)S(1)} %all_to_all.15.got.got_tile, f32[16,48,128]{2,1,0:T(8,128)S(1)} %all_to_all.16.got_grp, f32[1,4,40,320]{3,2,1,0:T(8,128)} %nest.3), custom_call_target="tpu_custom_call" | custom-call | tf_op jit(solution)/shard_map/fine/pallas_call | solution.py:395
  45.7 4.2 %all-to-all-start.2 = ((f32[128,4,128]{2,1,0:T(4,128)}), f32[128,4,128]{2,1,0:T(4,128)S(1)}, u32[]{:S(2)}, u32[]{:S(2)}) async-start(f32[128,4,128]{2,1,0:T(4,128)} %get-tuple-element.8), calls=%async_computation.2 | async-start | bytes 524288 | tf_op jit(solution)/shard_map/all_to_all | solution.py:429
  49.9 2.1 %step.1.stepped = f32[4,64,128]{2,1,0:T(8,128)} custom-call(f32[8,168,128]{2,1,0:T(8,128)S(1)} %all_to_all.15.got.got_tile, f32[16,48,128]{2,1,0:T(8,128)S(1)} %all_to_all.16.got_grp, f32[4,64,128]{2,1,0:T(8,128)} %so2.3, f32[4,64,128]{2,1,0:T(8,128)} %east.3, f32[4,64,128]{2,1,0:T(8,128)} %north.3, f32[4,64,128]{2,1,0:T(8,128)} %diff.3), custom_call_target="tpu_custom_call" | custom-call | tf_op jit(solution)/shard_map/step/pallas_call | solution.py:421
  52.1 9.1 %all-to-all-done.2 = f32[128,4,128]{2,1,0:T(4,128)S(1)} async-done(((f32[128,4,128]{2,1,0:T(4,128)}), f32[128,4,128]{2,1,0:T(4,128)S(1)}, u32[]{:S(2)}, u32[]{:S(2)}) %all-to-all-start.2) | async-done | bytes 262176 | tf_op jit(solution)/shard_map/all_to_all | solution.py:429
  61.1 0.7 %place.1 = f32[4,64,128]{2,1,0:T(8,128)} custom-call(s32[16]{0:T(128)} %rows.7, s32[16]{0:T(128)} %offs.3, s32[16]{0:T(128)} %left.7, s32[16]{0:T(128)} %height.3, s32[16]{0:T(128)} %width.3, f32[4,64,128]{2,1,0:T(8,128)} %step.1.stepped, f32[16,32,128]{2,1,0:T(8,128)S(1)} %bitcast.1), custom_call_target="tpu_custom_call", output_to_operand_aliasing={{}: (5, {})} | custom-call | tf_op jit(solution)/shard_map/place/pallas_call | solution.py:431
Async XLA Ops:
  45.7 15.5 %all-to-all-start.2 = ((f32[128,4,128]{2,1,0:T(4,128)}), f32[128,4,128]{2,1,0:T(4,128)S(1)}, u32[]{:S(2)}, u32[]{:S(2)}) async-start(f32[128,4,128]{2,1,0:T(4,128)} %get-tuple-element.8), calls=%async_computation.2 | async-start | bytes 524288 | tf_op jit(solution)/shard_map/all_to_all | solution.py:429
where the time goes:
time: 63 us; the launch traced here: 61.9 us
  blocking collectives  35.6 us (57%)
  Pallas kernels  12.3 us (20%)
  waiting for transfers between devices  9.08 us (14%)
  starting transfers between devices  4.24 us (7%)
  between operations  0.67 us (1%)
    all_to_all x1, blocking collectives, shards(): got_tile = near(lax.all_to_all(send, 'tile', 0, 0))  20.7 us
    all_to_all x1, blocking collectives, shards(): got_grp = near(lax.all_to_all(send, 'grp', 0, 0))  14.9 us
    all_to_all x1, waiting for transfers between devices, shards(): got = lax.all_to_all(back, ('grp', 'tile'), 0, 0)  9.08 us
    pallas_call x1, Pallas kernels, shards(): pl.pallas_call(fine_kernel, out_shape=(shape((1, LEV, OWN, WIDE), f32), f...  6.45 us
    all_to_all x1, starting transfers between devices, shards(): got = lax.all_to_all(back, ('grp', 'tile'), 0, 0)  4.24 us
    pallas_call x1, Pallas kernels, shards(): pl.pallas_call(pack_kernel, out_shape=(field((TILES, WIN + 8 + HALO, 128)...  2.3 us
    pallas_call x1, Pallas kernels, shards(): pl.pallas_call(step_kernel, out_shape=shape((LEV, ROWS, COLS), f32), in_s...  2.13 us
  transfers between devices with their start and end apart: 1, of which 1 were waited for; matrix products, arithmetic and copies ran while one was open for 0% of the time, Pallas kernels for 3%

commit v1 on v0

v1 whole, which is shorter than its diff:
```python
import functools
import jax
import jax.numpy as jnp
from jax import lax
from jax.experimental import pallas as pl
from jax.experimental.pallas import tpu as pltpu
from jax.sharding import PartitionSpec as P

RATIO = 10
FR = 32
LEV = 4
ROWS = 64
COLS = 128
OWN = 40
WIDE = 320
GROUPS = 16
TILES = 8
SPAN = FR + 2
WIN = 30
EDGE = 34
SLOT = 136
GSLOT = 40
STARTS = (-1, 107, 215)
TAKEN = (0, 117, 225, 320)
MIX = 0.02

SMEM = pl.BlockSpec(memory_space=pltpu.SMEM)
ANY = pl.BlockSpec(memory_space=pl.ANY)
VMEM = pl.BlockSpec(memory_space=pltpu.VMEM)


def nest_over(rows, group):
    found = jnp.int32(0)
    for i in range(GROUPS):
        found = jnp.where(rows[i] == group, jnp.int32(i), found)
    return found


def lanes(shape):
    return lax.broadcasted_iota(jnp.int32, shape, 1)


def pack_kernel(rows, offs, left, so2, east, north, diff, nest, send, edges, x, nx, sems):
    t = lax.axis_index("tile")
    g = lax.axis_index("grp")
    loads = [
        pltpu.make_async_copy(f, x.at[pl.ds(4 * i, 4), pl.ds(0, ROWS), :], sems.at[i])
        for i, f in enumerate((so2, east, north, diff))
    ]
    loads.append(pltpu.make_async_copy(nest.at[0], nx, sems.at[4]))
    for c in loads:
        c.start()
    n = nest_over(rows, g)
    top = offs[n] - 1
    base = 128 * t + 1 - left[n] + 1024
    x[:, ROWS : ROWS + 8, :] = jnp.zeros((16, 8, 128), jnp.float32)
    lane = lanes((8, 128))
    before = jnp.where(t > 0, t - 1, t + 2)
    after = jnp.where(t < TILES - 1, t + 1, t - 2)
    loads[4].wait()
    for at, source in ((before, 0), (after, OWN - 10)):
        q = slice(source, source + 10)
        for l in range(LEV):
            for m in range(2):
                send[at, pl.ds(EDGE + 10 * (2 * l + m), 10), :] = nx[l, q, 128 * m : 128 * m + 128]
            side = 64 * (l % 2)
            send[at, pl.ds(EDGE + 80 + 10 * (l // 2), 10), side : side + 64] = nx[l, q, 256:320]
    for c in loads[:4]:
        c.wait()
    for l in range(LEV):
        edges[l : l + 1, :] = x[l, 0:1, :]
        edges[4 + l : 5 + l, :] = x[4 + l, 0:1, :]
        edges[8 + l : 9 + l, :] = x[l, ROWS - 1 : ROWS, :]
        edges[12 + l : 13 + l, :] = x[4 + l, ROWS - 1 : ROWS, :]
    first = jnp.zeros((8, 128), jnp.float32)
    last = jnp.zeros((8, 128), jnp.float32)
    for p in range(8):
        plane = p if p < 4 else p + 4
        for b in range(8):
            k = 8 * p + b
            v = x[plane, 8 * b : 8 * b + 8, :]
            first = jnp.where(lane == k, pltpu.roll(v, k, 1), first)
            last = jnp.where(lane == k, pltpu.roll(v, k + 1, 1), last)
    first = jnp.where(lane[0:4] < 64, first[0:4], pltpu.roll(first, 64, 1)[4:8])
    last = jnp.where(lane[0:4] < 64, last[0:4], pltpu.roll(last, 64, 1)[4:8])
    shifts = [lax.rem(base + SPAN * f, 128) for f in range(3)]
    kshifts = [lax.rem(base + 32 * l - 1, 128) for l in range(LEV)]
    for d in range(TILES):
        for l in range(LEV):
            part = [
                pltpu.roll(x[4 * f + l, pl.ds(top + 4 * d, 8), :], shifts[f], 1) for f in range(3)
            ]
            piece = jnp.where(lane < SPAN, part[0], jnp.where(lane < 2 * SPAN, part[1], part[2]))
            send[d, 6 * l : 6 * l + 6, :] = piece[0:6]
        part = [pltpu.roll(x[12 + l, pl.ds(top + 4 * d, 8), :], kshifts[l], 1) for l in range(LEV)]
        piece = jnp.where(
            lane < 64,
            jnp.where(lane < 32, part[0], part[1]),
            jnp.where(lane < 96, part[2], part[3]),
        )
        send[d, 24:WIN, :] = piece[0:6]
        send[d, WIN:EDGE, :] = jnp.where(d < t, first, last)


def merge_kernel(rows, left, got, edges, send):
    g = lax.axis_index("grp")
    n = nest_over(rows, g)
    start = left[n] - 1
    first = lax.div(start, COLS)
    second = jnp.minimum(first + 1, TILES - 1)
    send[jnp.where(g > 0, g - 1, g + 2), WIN : WIN + 8, :] = edges[0:8, :]
    send[jnp.where(g < GROUPS - 1, g + 1, g - 2), WIN : WIN + 8, :] = edges[8:16, :]
    room = COLS - (start - COLS * first)
    lane = lanes((8, 128))
    col = lane - jnp.where(lane >= SPAN, SPAN, 0) - jnp.where(lane >= 2 * SPAN, SPAN, 0)
    kcol = (lane & 31) + 1
    for l in range(3):
        q = slice(8 * l, 8 * l + 8)
        send[n, q, :] = jnp.where(col < room, got[first, q, :], got[second, q, :])
    q = slice(24, WIN)
    send[n, q, :] = jnp.where(kcol[0:6] < room, got[first, q, :], got[second, q, :])


def pos(v):
    return jnp.maximum(v, 0.0)


def neg(v):
    return jnp.minimum(v, 0.0)


def fine_kernel(
    rows, left, height, width, got_tile, got_grp, nest,
    c, back,
    nx, third, e, raw, am, ap, bm, bp, ac, kz, sums, sems,
):
    t = lax.axis_index("tile")
    g = lax.axis_index("grp")
    src = rows[g]
    prev_t = jnp.maximum(t - 1, 0)
    next_t = jnp.minimum(t + 1, TILES - 1)
    load = pltpu.make_async_copy(nest.at[0], nx, sems.at[0])
    load.start()
    lane = lanes((8, 128))
    sub = lax.broadcasted_iota(jnp.int32, (8, 128), 0)
    zero = jnp.zeros((8, 128), jnp.float32)
    for l in range(LEV):
        for m in range(3):
            raw[l, m, 56:64, :] = zero
            for p in range(2):
                c[p, l, m, 0:8, :] = zero
                c[p, l, m, 72:80, :] = zero

    above = OWN // RATIO * t - 1 + sub
    row_in = (above >= 0) & (above < height[g])
    coarse = {}
    for m in range(3):
        col = STARTS[m] + lane
        under = (jnp.maximum(col, 0) * 6554) >> 16
        pick = jnp.where(col < 0, 0, jnp.where(col < WIDE, under + 1, SPAN - 1))
        kpick = jnp.minimum(under, FR - 1)
        inside = row_in & (col >= 0) & (col < RATIO * width[g])
        block = got_grp[src, 24:32, :]
        ks = [jnp.take_along_axis(block, kpick + 32 * l, axis=1) for l in range(LEV)]
        faces = [0.05 * (ks[l] + ks[l + 1]) for l in range(LEV - 1)]
        for l in range(LEV - 1):
            e[10 * LEV + l, m] = jnp.where(inside, faces[l], 0.0)
        for l in range(LEV):
            block = got_grp[src, 6 * l : 6 * l + 8, :]
            e[l, m] = jnp.take_along_axis(block, pick, axis=1)
            u = jnp.take_along_axis(block, pick + SPAN, axis=1)
            v = jnp.take_along_axis(block, pick + 2 * SPAN, axis=1)
            u_lo = 0.5 * (pltpu.roll(u, 1, 0) + u)
            u_hi = 0.5 * (u + pltpu.roll(u, 7, 0))
            v_lo = 0.5 * (pltpu.roll(v, 1, 1) + v)
            v_hi = 0.5 * (v + pltpu.roll(v, 127, 1))
            rest = (1.0 - 4.0 * MIX) - pos(v_hi) + neg(v_lo)
            if l > 0:
                rest = rest - faces[l - 1]
            if l < LEV - 1:
                rest = rest - faces[l]
            values = (
                rest - pos(u) + neg(u),
                rest - pos(u) + neg(u_lo),
                rest - pos(u_hi) + neg(u),
                MIX + pos(u),
                MIX + pos(u_lo),
                MIX - neg(u),
                MIX - neg(u_hi),
                MIX + pos(v_lo),
                MIX - neg(v_hi),
            )
            for k, value in enumerate(values):
                e[LEV * (k + 1) + l, m] = jnp.where(inside, value, 1.0 if k < 3 else 0.0)

    def spread(p, m, i):
        lo, hi = (8 * i) // 10, min((8 * i + 7) // 10, 5)
        low = jnp.broadcast_to(e[p, m, lo : lo + 1, :], (8, 128))
        if lo == hi:
            return low
        high = jnp.broadcast_to(e[p, m, hi : hi + 1, :], (8, 128))
        return jnp.where(sub < 10 * hi - 8 * i, low, high)

    def at_row(value, p, m, i, last):
        for k in range(6):
            at = 10 * k + (9 if last else 0) - 8 * i
            if 0 <= at < 8:
                value = jnp.where(sub == at, jnp.broadcast_to(e[p, m, k : k + 1, :], (8, 128)), value)
        return value

    for i in range(8):
        q = slice(8 * i, 8 * i + 8)
        for m in range(3):
            for l in range(LEV - 1):
                kz[l, m, q, :] = spread(10 * LEV + l, m, i)
            for l in range(LEV):
                mid = at_row(spread(LEV + l, m, i), 2 * LEV + l, m, i, False)
                ac[l, m, q, :] = at_row(mid, 3 * LEV + l, m, i, True)
                am[l, m, q, :] = at_row(spread(4 * LEV + l, m, i), 5 * LEV + l, m, i, False)
                ap[l, m, q, :] = at_row(spread(6 * LEV + l, m, i), 7 * LEV + l, m, i, True)
                bm[l, m, q, :] = spread(8 * LEV + l, m, i)
                bp[l, m, q, :] = spread(9 * LEV + l, m, i)

    load.wait()

    def lay(l, at, n, parts, turn):
        wide = lanes((n, 128))
        raw[l, 0, at : at + n, :] = pltpu.roll(parts[0], 1, 1)
        raw[l, 1, at : at + n, :] = jnp.where(
            wide < 21, pltpu.roll(parts[0], 21, 1), pltpu.roll(parts[1], 21, 1)
        )
        raw[l, 2, at : at + n, :] = jnp.where(
            wide < 41, pltpu.roll(parts[1], 41, 1), pltpu.roll(parts[2], turn, 1)
        )

    for l in range(LEV):
        third[l, :, 0:64] = nx[l, :, 256:320]
        lay(l, 10, OWN, (nx[l, :, 0:128], nx[l, :, 128:256], third[l]), 41)
        turn = 41 if l % 2 == 0 else 105
        for tile, at in ((prev_t, 0), (next_t, OWN + 10)):
            spots = (EDGE + 20 * l, EDGE + 20 * l + 10, EDGE + 80 + 10 * (l // 2))
            lay(l, at, 10, [got_tile[tile, k : k + 10, :] for k in spots], turn)
    last_row = RATIO * height[g]
    first_row = OWN * t - 10
    for i in range(8):
        r = 8 + 8 * i
        row = first_row + 8 * i + sub
        row_in = (row >= 0) & (row < last_row)
        for m in range(3):
            col = STARTS[m] + lane
            active = row_in & (col >= 0) & (col < RATIO * width[g])
            for l in range(LEV):
                c[0, l, m, r : r + 8, :] = jnp.where(active, raw[l, m, r - 8 : r, :], spread(l, m, i))

    def advance(old, new, tiles):
        for m in range(3):
            for i in tiles:
                r = 8 + 8 * i
                q = slice(8 * i, 8 * i + 8)
                now = [c[old, l, m, r : r + 8, :] for l in range(LEV)]
                flow = [kz[l, m, q, :] for l in range(LEV - 1)]
                for l in range(LEV):
                    value = ac[l, m, q, :] * now[l]
                    value = value + am[l, m, q, :] * c[old, l, m, r - 1 : r + 7, :]
                    value = value + ap[l, m, q, :] * c[old, l, m, r + 1 : r + 9, :]
                    value = value + bm[l, m, q, :] * pltpu.roll(now[l], 1, 1)
                    value = value + bp[l, m, q, :] * pltpu.roll(now[l], 127, 1)
                    if l > 0:
                        value = value + flow[l - 1] * now[l - 1]
                    if l < LEV - 1:
                        value = value + flow[l] * now[l + 1]
                    c[new, l, m, r : r + 8, :] = value

    def steps(first, last, tiles):
        def body(k, carry):
            old = lax.rem(k, 2)
            advance(old, 1 - old, tiles)
            return carry

        lax.fori_loop(first, last, body, 0)

    steps(0, 3, range(8))
    steps(3, 7, range(7))
    steps(7, RATIO, range(1, 7))
    for l in range(LEV):
        for m in range(3):
            for a in range(4):
                band = c[0, l, m, 18 + 10 * a : 28 + 10 * a, :]
                sums[m, 4 * l + a : 4 * l + a + 1, :] = jnp.sum(band, axis=0, keepdims=True)
    mean = jnp.zeros((16, 128), jnp.float32)
    for m in range(3):
        col = STARTS[m] + lax.broadcasted_iota(jnp.int32, (128, 128), 0)
        chosen = ((jnp.maximum(col, 0) * 6554) >> 16) == lanes((128, 128))
        chosen = chosen & (col >= TAKEN[m]) & (col < TAKEN[m + 1])
        pick = jnp.where(chosen, 1.0, 0.0)
        mean = mean + jnp.dot(
            sums[m], pick, precision=lax.Precision.HIGHEST, preferred_element_type=jnp.float32
        )
    mean = mean * (1.0 / (RATIO * RATIO))
    lane4 = lanes((4, 128))
    value = jnp.zeros((4, 128), jnp.float32)
    turned = [mean if l == 0 else pltpu.roll(mean, 32 * l, 1) for l in range(LEV)]
    for l in range(LEV):
        inside = (lane4 >= 32 * l) & (lane4 < 32 * l + 32)
        value = jnp.where(inside, turned[l][4 * l : 4 * l + 4, :], value)
    tile_a = lax.div(left[g], COLS)
    tile_b = jnp.where(tile_a < TILES - 1, tile_a + 1, tile_a - 1)
    back[TILES * src + tile_a] = value
    back[TILES * src + tile_b] = value


def finish_kernel(got_tile, got_grp, c, so2, east, north, diff, stepped, fine_out, px, vk, ed, sems):
    t = lax.axis_index("tile")
    g = lax.axis_index("grp")
    prev_t = jnp.maximum(t - 1, 0)
    next_t = jnp.minimum(t + 1, TILES - 1)
    prev_g = jnp.maximum(g - 1, 0)
    next_g = jnp.minimum(g + 1, GROUPS - 1)
    copies = [
        (so2, px.at[pl.ds(0, 4), pl.ds(8, ROWS), :]),
        (east, px.at[pl.ds(4, 4), pl.ds(8, ROWS), :]),
        (north, vk.at[pl.ds(0, 4)]),
        (diff, vk.at[pl.ds(4, 4)]),
    ]
    copies = [pltpu.make_async_copy(s, d, sems.at[i]) for i, (s, d) in enumerate(copies)]
    for copy in copies:
        copy.start()
    lane = lanes((8, 128))
    wide = lanes((OWN, 128))
    for l in range(LEV):
        turned = [pltpu.roll(c[0, l, m, 18:58, :], by, 1) for m, by in enumerate((127, 107, 87))]
        fine_out[0, l, :, 0:128] = jnp.where(wide < 117, turned[0], turned[1])
        fine_out[0, l, :, 128:256] = jnp.where(wide < 97, turned[1], turned[2])
        fine_out[0, l, :, 256:320] = turned[2][:, 0:64]
    for copy in copies:
        copy.wait()
    for p in range(8):
        px[p, 7:8, :] = jnp.where(g > 0, got_grp[prev_g, WIN + p : WIN + p + 1, :], 0.0)
        px[p, 72:73, :] = jnp.where(g < GROUPS - 1, got_grp[next_g, WIN + p : WIN + p + 1, :], 0.0)
    for k, tile in enumerate((prev_t, next_t)):
        packed = got_tile[tile, WIN : WIN + 8, :]
        ed[k, 0:4, :] = packed[0:4]
        ed[k, 4:8, :] = pltpu.roll(packed, 64, 1)[0:4]
    edge_l = jnp.where(t > 0, ed[0], 0.0)
    edge_r = jnp.where(t < TILES - 1, ed[1], 0.0)
    for b in range(8):
        r = 8 + 8 * b
        q = slice(8 * b, 8 * b + 8)
        now = [px[l, r : r + 8, :] for l in range(LEV)]
        ks = [vk[4 + l, q, :] for l in range(LEV)]
        between = [0.5 * (ks[l] + ks[l + 1]) * (now[l + 1] - now[l]) for l in range(LEV - 1)]
        for l in range(LEV):
            here = now[l]
            k, kv = 8 * l + b, 32 + 8 * l + b
            wind = vk[l, q, :]
            c_w = jnp.where(lane == 0, pltpu.roll(edge_l, (128 - k) % 128, 1), pltpu.roll(here, 1, 1))
            c_e = jnp.where(lane == 127, pltpu.roll(edge_r, 127 - k, 1), pltpu.roll(here, 127, 1))
            v_w = jnp.where(lane == 0, pltpu.roll(edge_l, 128 - kv, 1), pltpu.roll(wind, 1, 1))
            v_e = jnp.where(lane == 127, pltpu.roll(edge_r, 127 - kv, 1), pltpu.roll(wind, 127, 1))
            c_n = px[l, r - 1 : r + 7, :]
            c_s = px[l, r + 1 : r + 9, :]
            flow = px[4 + l, r : r + 8, :]
            u_lo = 0.5 * (px[4 + l, r - 1 : r + 7, :] + flow)
            u_hi = 0.5 * (flow + px[4 + l, r + 1 : r + 9, :])
            v_lo = 0.5 * (v_w + wind)
            v_hi = 0.5 * (wind + v_e)
            value = (
                here
                - ((pos(u_hi) * here + neg(u_hi) * c_s) - (pos(u_lo) * c_n + neg(u_lo) * here))
                - ((pos(v_hi) * here + neg(v_hi) * c_e) - (pos(v_lo) * c_w + neg(v_lo) * here))
                + MIX * (c_n + c_s + c_w + c_e - 4.0 * here)
            )
            if l < LEV - 1:
                value = value + between[l]
            if l > 0:
                value = value - between[l - 1]
            stepped[l, q, :] = value


def place_kernel(rows, offs, left, height, width, stepped, got, out, s, sems):
    t = lax.axis_index("tile")
    g = lax.axis_index("grp")
    n = nest_over(rows, g)
    lf = left[n]
    wd = width[n]

    @pl.when((lf < COLS * t + COLS) & (lf + wd > COLS * t))
    def _():
        off = offs[n]
        base = pl.multiple_of(lax.div(off, 8) * 8, 8)
        load_s = pltpu.make_async_copy(stepped.at[:, pl.ds(base, 40), :], s, sems.at[0])
        load_s.start()
        lane = lanes((FR, 128)) + COLS * t
        row = lax.broadcasted_iota(jnp.int32, (FR, 128), 0)
        covered = (lane >= lf) & (lane < lf + wd) & (row < height[n])
        load_s.wait()
        for l in range(LEV):
            turned = pltpu.roll(got[n], lax.rem(lf - COLS * t - 32 * l + 2048, 128), 1)
            at = pl.ds(off - base, FR)
            s[l, at, :] = jnp.where(covered, turned, s[l, at, :])
        store = pltpu.make_async_copy(s, out.at[:, pl.ds(base, 40), :], sems.at[1])
        store.start()
        store.wait()


def shards(so2, east, north, diff, nest, rows, offs, left, height, width):
    f32 = jnp.float32
    shape = jax.ShapeDtypeStruct
    dma = pltpu.SemaphoreType.DMA
    field = functools.partial(pltpu.VMEM, dtype=f32)
    near = functools.partial(pltpu.with_memory_space_constraint, memory_space=pltpu.VMEM)
    send, edges = pl.pallas_call(
        pack_kernel,
        out_shape=(field((TILES, SLOT, 128)), field((16, 128))),
        in_specs=[SMEM] * 3 + [ANY] * 5,
        out_specs=(VMEM, VMEM),
        scratch_shapes=[field((16, ROWS + 8, 128)), field((LEV, OWN, WIDE)), dma((5,))],
        name="pack",
    )(rows, offs, left, so2, east, north, diff, nest)
    got_tile = near(lax.all_to_all(send, "tile", 0, 0))
    send = pl.pallas_call(
        merge_kernel,
        out_shape=field((GROUPS, GSLOT, 128)),
        in_specs=[SMEM] * 2 + [VMEM, VMEM],
        out_specs=VMEM,
        name="merge",
    )(rows, left, got_tile, near(edges))
    got_grp = near(lax.all_to_all(send, "grp", 0, 0))
    c, back = pl.pallas_call(
        fine_kernel,
        out_shape=(field((2, LEV, 3, 80, 128)), field((GROUPS * TILES, 4, 128))),
        in_specs=[SMEM] * 4 + [VMEM] * 2 + [ANY],
        out_specs=(VMEM, VMEM),
        scratch_shapes=[
            field((LEV, OWN, WIDE)),
            field((LEV, OWN, 128)),
            field((11 * LEV - 1, 3, 8, 128)),
            field((LEV, 3, 64, 128)),
            field((LEV, 3, 64, 128)),
            field((LEV, 3, 64, 128)),
            field((LEV, 3, 64, 128)),
            field((LEV, 3, 64, 128)),
            field((LEV, 3, 64, 128)),
            field((LEV - 1, 3, 64, 128)),
            field((3, 16, 128)),
            dma((1,)),
        ],
        name="fine",
    )(rows, left, height, width, got_tile, got_grp, nest)
    stepped, nest_next = pl.pallas_call(
        finish_kernel,
        out_shape=(shape((LEV, ROWS, COLS), f32), shape((1, LEV, OWN, WIDE), f32)),
        in_specs=[VMEM] * 3 + [ANY] * 4,
        out_specs=(VMEM, VMEM),
        scratch_shapes=[
            field((8, ROWS + 16, 128)),
            field((8, ROWS, 128)),
            field((2, 8, 128)),
            dma((4,)),
        ],
        name="finish",
    )(got_tile, got_grp, near(c), so2, east, north, diff)
    got = lax.all_to_all(back, ("grp", "tile"), 0, 0)
    got = near(got.reshape(GROUPS, FR, 128))
    parent_next = pl.pallas_call(
        place_kernel,
        out_shape=shape((LEV, ROWS, COLS), f32),
        in_specs=[SMEM] * 5 + [ANY, VMEM],
        out_specs=ANY,
        scratch_shapes=[field((LEV, 40, 128)), dma((2,))],
        input_output_aliases={5: 0},
        name="place",
    )(rows, offs, left, height, width, stepped, got)
    return parent_next, nest_next


def solution(mesh):
    in_specs = (
        P(None, "grp", "tile"),
        P(None, "grp", "tile"),
        P(None, "grp", "tile"),
        P(None, "grp", "tile"),
        P("grp", None, "tile", None),
        P(),
        P(),
        P(),
        P(),
        P(),
    )
    out_specs = (P(None, "grp", "tile"), P("grp", None, "tile", None))
    return jax.shard_map(shards, mesh=mesh, in_specs=in_specs, out_specs=out_specs, check_vma=False)
```

time: 63 us -> 61.8 us (0.981); the launches traced: 61.9 us -> 62.3 us
  Pallas kernels: 12.3 us -> 14.8 us
  blocking collectives: 35.6 us -> 33.8 us
    all_to_all x1, blocking collectives: 20.7 us -> 18.9 us  [shards(): got_tile = near(lax.all_to_all(send, 'tile', 0, 0))]
    pallas_call x1, Pallas kernels: 0.74 us -> 2.35 us  [shards(): pl.pallas_call(place_kernel, out_shape=shape((LEV, ROWS, COLS), f32), in_...]
    pallas_call x4, Pallas kernels: 11.6 us -> 12.4 us  [the longest x1 7.06 us: shards(): pl.pallas_call(fine_kernel, out_shape=(field((2, LEV, 3, 80, 128)), field...]
  transfers between devices with their start and end apart: 1 -> 1, of which waited for: 1 -> 1; matrix products, arithmetic and copies ran while one was open for 0% -> 0% of each run, Pallas kernels for 3% -> 4%
where the time goes in v1:
time: 61.8 us; the launch traced here: 62.3 us
  blocking collectives  33.8 us (55%)
  Pallas kernels  14.8 us (24%)
  waiting for transfers between devices  9.09 us (15%)
  starting transfers between devices  3.91 us (6%)
  between operations  0.67 us (1%)
    all_to_all x1, blocking collectives, shards(): got_tile = near(lax.all_to_all(send, 'tile', 0, 0))  18.9 us
    all_to_all x1, blocking collectives, shards(): got_grp = near(lax.all_to_all(send, 'grp', 0, 0))  14.9 us
    all_to_all x1, waiting for transfers between devices, shards(): got = lax.all_to_all(back, ('grp', 'tile'), 0, 0)  9.09 us
    pallas_call x1, Pallas kernels, shards(): pl.pallas_call(fine_kernel, out_shape=(field((2, LEV, 3, 80, 128)), field...  7.06 us
    all_to_all x1, starting transfers between devices, shards(): got = lax.all_to_all(back, ('grp', 'tile'), 0, 0)  3.91 us
    pallas_call x1, Pallas kernels, shards(): pl.pallas_call(pack_kernel, out_shape=(field((TILES, SLOT, 128)), field((...  2.43 us
    pallas_call x1, Pallas kernels, shards(): pl.pallas_call(place_kernel, out_shape=shape((LEV, ROWS, COLS), f32), in_...  2.35 us
    pallas_call x1, Pallas kernels, shards(): pl.pallas_call(finish_kernel, out_shape=(shape((LEV, ROWS, COLS), f32), s...  2.24 us
  transfers between devices with their start and end apart: 1, of which 1 were waited for; matrix products, arithmetic and copies ran while one was open for 0% of the time, Pallas kernels for 4%

profile of v1, /device:TPU:1, one launch (start us, length us, event | category | flops | bytes accessed | tf_op | source)
XLA Modules:
  0.0 62.3 jit_solution(4657651754424645300)
XLA Ops:
  0.6 2.4 %pack.1 = (f32[8,136,128]{2,1,0:T(8,128)S(1)}, f32[16,128]{1,0:T(8,128)S(1)}) custom-call(s32[16]{0:T(128)} %rows.7, s32[16]{0:T(128)} %offs.3, s32[16]{0:T(128)} %left.7, f32[4,64,128]{2,1,0:T(8,128)} %so2.3, f32[4,64,128]{2,1,0:T(8,128)} %east.3, f32[4,64,128]{2,1,0:T(8,128)} %north.3, f32[4,64,128]{2,1,0:T(8,128)} %diff.3, f32[1,4,40,320]{3,2,1,0:T(8,128)} %nest.3), custom_call_target="tpu_custom_call" | custom-call | tf_op jit(solution)/shard_map/pack/pallas_call | solution.py:412
  3.1 18.9 %all_to_all.15.got.got_tile = f32[8,136,128]{2,1,0:T(8,128)S(1)} all-to-all(f32[8,136,128]{2,1,0:T(8,128)S(1)} %get-tuple-element.8), channel_id=1, replica_groups=mesh['grp'=16,'tile'=8] {'tile'}, dimensions={0} | all-to-all | bytes 1114112 | tf_op jit(solution)/shard_map/all_to_all | solution.py:420
  22.0 0.7 %merge.1 = f32[16,40,128]{2,1,0:T(8,128)S(1)} custom-call(s32[16]{0:T(128)} %rows.7, s32[16]{0:T(128)} %left.7, f32[8,136,128]{2,1,0:T(8,128)S(1)} %all_to_all.15.got.got_tile, f32[16,128]{1,0:T(8,128)S(1)} %get-tuple-element.9.edges), custom_call_target="tpu_custom_call" | custom-call | tf_op jit(solution)/shard_map/merge/pallas_call | solution.py:421
  22.7 14.9 %all_to_all.16.got_grp = f32[16,40,128]{2,1,0:T(8,128)S(1)} all-to-all(f32[16,40,128]{2,1,0:T(8,128)S(1)} %merge.1), channel_id=1, replica_groups=mesh['grp'=16,'tile'=8] {'grp'}, dimensions={0} | all-to-all | bytes 655360 | tf_op jit(solution)/shard_map/all_to_all | solution.py:428
  37.6 7.1 %fine.1 = (f32[2,4,3,80,128]{4,3,2,1,0:T(8,128)S(1)}, f32[128,4,128]{2,1,0:T(4,128)}) custom-call(s32[16]{0:T(128)} %rows.7, s32[16]{0:T(128)} %left.7, s32[16]{0:T(128)} %height.3, s32[16]{0:T(128)} %width.3, f32[8,136,128]{2,1,0:T(8,128)S(1)} %all_to_all.15.got.got_tile, f32[16,40,128]{2,1,0:T(8,128)S(1)} %all_to_all.16.got_grp, f32[1,4,40,320]{3,2,1,0:T(8,128)} %nest.3), custom_call_target="tpu_custom_call" | custom-call | tf_op jit(solution)/shard_map/fine/pallas_call | solution.py:429
  44.7 3.9 %all-to-all-start.2 = ((f32[128,4,128]{2,1,0:T(4,128)}), f32[128,4,128]{2,1,0:T(4,128)S(1)}, u32[]{:S(2)}, u32[]{:S(2)}) async-start(f32[128,4,128]{2,1,0:T(4,128)} %get-tuple-element.12), calls=%async_computation.2 | async-start | bytes 524288 | tf_op jit(solution)/shard_map/all_to_all | solution.py:463
  48.6 2.2 %finish.1 = (f32[4,64,128]{2,1,0:T(8,128)}, f32[1,4,40,320]{3,2,1,0:T(8,128)}) custom-call(f32[8,136,128]{2,1,0:T(8,128)S(1)} %all_to_all.15.got.got_tile, f32[16,40,128]{2,1,0:T(8,128)S(1)} %all_to_all.16.got_grp, f32[2,4,3,80,128]{4,3,2,1,0:T(8,128)S(1)} %get-tuple-element.10.c, f32[4,64,128]{2,1,0:T(8,128)} %so2.3, f32[4,64,128]{2,1,0:T(8,128)} %east.3, ...), custom_call_target="tpu_custom_call" | custom-call | tf_op jit(solution)/shard_map/finish/pallas_call | solution.py:450
  50.8 9.1 %all-to-all-done.2 = f32[128,4,128]{2,1,0:T(4,128)S(1)} async-done(((f32[128,4,128]{2,1,0:T(4,128)}), f32[128,4,128]{2,1,0:T(4,128)S(1)}, u32[]{:S(2)}, u32[]{:S(2)}) %all-to-all-start.2) | async-done | bytes 262176 | tf_op jit(solution)/shard_map/all_to_all | solution.py:463
  59.9 2.4 %place.1 = f32[4,64,128]{2,1,0:T(8,128)} custom-call(s32[16]{0:T(128)} %rows.7, s32[16]{0:T(128)} %offs.3, s32[16]{0:T(128)} %left.7, s32[16]{0:T(128)} %height.3, s32[16]{0:T(128)} %width.3, f32[4,64,128]{2,1,0:T(8,128)} %get-tuple-element.11.stepped, f32[16,32,128]{2,1,0:T(8,128)S(1)} %bitcast.1), custom_call_target="tpu_custom_call", output_to_operand_aliasing={{}: (5, {})} | custom-call | tf_op jit(solution)/shard_map/place/pallas_call | solution.py:465
Async XLA Ops:
  44.7 15.3 %all-to-all-start.2 = ((f32[128,4,128]{2,1,0:T(4,128)}), f32[128,4,128]{2,1,0:T(4,128)S(1)}, u32[]{:S(2)}, u32[]{:S(2)}) async-start(f32[128,4,128]{2,1,0:T(4,128)} %get-tuple-element.12), calls=%async_computation.2 | async-start | bytes 524288 | tf_op jit(solution)/shard_map/all_to_all | solution.py:463

commit v2 on v1

--- a/solution.py
+++ b/solution.py
@@ -20,8 +20,8 @@
 EDGE = 34
 SLOT = 136
 GSLOT = 40
-STARTS = (-1, 107, 215)
-TAKEN = (0, 117, 225, 320)
+STARTS = (0, 96, 192)
+TAKEN = (0, 117, 203, 320)
 MIX = 0.02
 
 SMEM = pl.BlockSpec(memory_space=pltpu.SMEM)
@@ -40,7 +40,7 @@
     return lax.broadcasted_iota(jnp.int32, shape, 1)
 
 
-def pack_kernel(rows, offs, left, so2, east, north, diff, nest, send, edges, x, nx, sems):
+def pack_kernel(rows, offs, left, so2, east, north, diff, nest, send, edges, x, nx, cut, sems):
     t = lax.axis_index("tile")
     g = lax.axis_index("grp")
     loads = [
@@ -72,34 +72,36 @@
         edges[4 + l : 5 + l, :] = x[4 + l, 0:1, :]
         edges[8 + l : 9 + l, :] = x[l, ROWS - 1 : ROWS, :]
         edges[12 + l : 13 + l, :] = x[4 + l, ROWS - 1 : ROWS, :]
-    first = jnp.zeros((8, 128), jnp.float32)
-    last = jnp.zeros((8, 128), jnp.float32)
-    for p in range(8):
-        plane = p if p < 4 else p + 4
-        for b in range(8):
-            k = 8 * p + b
-            v = x[plane, 8 * b : 8 * b + 8, :]
-            first = jnp.where(lane == k, pltpu.roll(v, k, 1), first)
-            last = jnp.where(lane == k, pltpu.roll(v, k + 1, 1), last)
-    first = jnp.where(lane[0:4] < 64, first[0:4], pltpu.roll(first, 64, 1)[4:8])
-    last = jnp.where(lane[0:4] < 64, last[0:4], pltpu.roll(last, 64, 1)[4:8])
     shifts = [lax.rem(base + SPAN * f, 128) for f in range(3)]
     kshifts = [lax.rem(base + 32 * l - 1, 128) for l in range(LEV)]
-    for d in range(TILES):
+    for b in range(5):
+        at = pl.ds(top + 8 * b, 8)
+        q = slice(8 * b, 8 * b + 8)
         for l in range(LEV):
-            part = [
-                pltpu.roll(x[4 * f + l, pl.ds(top + 4 * d, 8), :], shifts[f], 1) for f in range(3)
-            ]
-            piece = jnp.where(lane < SPAN, part[0], jnp.where(lane < 2 * SPAN, part[1], part[2]))
-            send[d, 6 * l : 6 * l + 6, :] = piece[0:6]
-        part = [pltpu.roll(x[12 + l, pl.ds(top + 4 * d, 8), :], kshifts[l], 1) for l in range(LEV)]
-        piece = jnp.where(
+            part = [pltpu.roll(x[4 * f + l, at, :], shifts[f], 1) for f in range(3)]
+            cut[l, q, :] = jnp.where(lane < SPAN, part[0], jnp.where(lane < 2 * SPAN, part[1], part[2]))
+        part = [pltpu.roll(x[12 + l, at, :], kshifts[l], 1) for l in range(LEV)]
+        cut[4, q, :] = jnp.where(
             lane < 64,
             jnp.where(lane < 32, part[0], part[1]),
             jnp.where(lane < 96, part[2], part[3]),
         )
-        send[d, 24:WIN, :] = piece[0:6]
-        send[d, WIN:EDGE, :] = jnp.where(d < t, first, last)
+    sub = lax.broadcasted_iota(jnp.int32, (8, 128), 0)
+    ends = jnp.where(((sub == 0) & (lane == 0)) | ((sub == 1) & (lane == 127)), 1.0, 0.0)
+    planes = [x[p if p < 4 else p + 4, 0:ROWS, :] for p in range(8)]
+    sides = lax.dot_general(
+        ends,
+        jnp.concatenate(planes, axis=0),
+        (((1,), (1,)), ((), ())),
+        precision=lax.Precision.HIGHEST,
+        preferred_element_type=jnp.float32,
+    )
+    for d in range(TILES):
+        for l in range(5):
+            send[d, 6 * l : 6 * l + 6, :] = cut[l, 4 * d : 4 * d + 6, :]
+        for k in range(4):
+            pair = sides[0:2, 128 * k : 128 * k + 128]
+            send[d, WIN + k : WIN + k + 1, :] = jnp.where(d < t, pair[0:1], pair[1:2])
 
 
 def merge_kernel(rows, left, got, edges, send):
@@ -121,6 +123,15 @@
     send[n, q, :] = jnp.where(kcol[0:6] < room, got[first, q, :], got[second, q, :])
 
 
+def columns(chunk, lane):
+    col = STARTS[chunk] + lane
+    if chunk == 0:
+        return jnp.where(lane == 127, -1, col)
+    if chunk == 2:
+        return jnp.where(lane == 0, WIDE, col)
+    return col
+
+
 def pos(v):
     return jnp.maximum(v, 0.0)
 
@@ -132,7 +143,7 @@
 def fine_kernel(
     rows, left, height, width, got_tile, got_grp, nest,
     c, back,
-    nx, third, e, raw, am, ap, bm, bp, ac, kz, sums, sems,
+    slot, nx, last_part, e, raw, am, ap, bm, bp, ac, kz, sums, sems,
 ):
     t = lax.axis_index("tile")
     g = lax.axis_index("grp")
@@ -155,7 +166,7 @@
     row_in = (above >= 0) & (above < height[g])
     coarse = {}
     for m in range(3):
-        col = STARTS[m] + lane
+        col = columns(m, lane)
         under = (jnp.maximum(col, 0) * 6554) >> 16
         pick = jnp.where(col < 0, 0, jnp.where(col < WIDE, under + 1, SPAN - 1))
         kpick = jnp.minimum(under, FR - 1)
@@ -225,21 +236,18 @@
 
     def lay(l, at, n, parts, turn):
         wide = lanes((n, 128))
-        raw[l, 0, at : at + n, :] = pltpu.roll(parts[0], 1, 1)
-        raw[l, 1, at : at + n, :] = jnp.where(
-            wide < 21, pltpu.roll(parts[0], 21, 1), pltpu.roll(parts[1], 21, 1)
-        )
-        raw[l, 2, at : at + n, :] = jnp.where(
-            wide < 41, pltpu.roll(parts[1], 41, 1), pltpu.roll(parts[2], turn, 1)
-        )
+        q = slice(at, at + n)
+        raw[l, 0, q, :] = parts[0]
+        raw[l, 1, q, :] = jnp.where(wide < 32, pltpu.roll(parts[0], 32, 1), pltpu.roll(parts[1], 32, 1))
+        third = pltpu.roll(parts[2], 64, 1) if turn else parts[2]
+        raw[l, 2, q, :] = jnp.where(wide < 64, pltpu.roll(parts[1], 64, 1), third)
 
     for l in range(LEV):
-        third[l, :, 0:64] = nx[l, :, 256:320]
-        lay(l, 10, OWN, (nx[l, :, 0:128], nx[l, :, 128:256], third[l]), 41)
-        turn = 41 if l % 2 == 0 else 105
+        last_part[l, :, 64:128] = nx[l, :, 256:320]
+        lay(l, 10, OWN, (nx[l, :, 0:128], nx[l, :, 128:256], last_part[l]), False)
         for tile, at in ((prev_t, 0), (next_t, OWN + 10)):
             spots = (EDGE + 20 * l, EDGE + 20 * l + 10, EDGE + 80 + 10 * (l // 2))
-            lay(l, at, 10, [got_tile[tile, k : k + 10, :] for k in spots], turn)
+            lay(l, at, 10, [got_tile[tile, k : k + 10, :] for k in spots], l % 2 == 0)
     last_row = RATIO * height[g]
     first_row = OWN * t - 10
     for i in range(8):
@@ -247,7 +255,7 @@
         row = first_row + 8 * i + sub
         row_in = (row >= 0) & (row < last_row)
         for m in range(3):
-            col = STARTS[m] + lane
+            col = columns(m, lane)
             active = row_in & (col >= 0) & (col < RATIO * width[g])
             for l in range(LEV):
                 c[0, l, m, r : r + 8, :] = jnp.where(active, raw[l, m, r - 8 : r, :], spread(l, m, i))
@@ -271,31 +279,36 @@
                         value = value + flow[l] * now[l + 1]
                     c[new, l, m, r : r + 8, :] = value
 
-    def steps(first, last, tiles):
-        def body(k, carry):
-            old = lax.rem(k, 2)
-            advance(old, 1 - old, tiles)
+    def steps(count, tiles):
+        def body(_, carry):
+            advance(0, 1, tiles)
+            advance(1, 0, tiles)
             return carry
 
-        lax.fori_loop(first, last, body, 0)
-
-    steps(0, 3, range(8))
-    steps(3, 7, range(7))
-    steps(7, RATIO, range(1, 7))
-    for l in range(LEV):
-        for m in range(3):
-            for a in range(4):
-                band = c[0, l, m, 18 + 10 * a : 28 + 10 * a, :]
-                sums[m, 4 * l + a : 4 * l + a + 1, :] = jnp.sum(band, axis=0, keepdims=True)
-    mean = jnp.zeros((16, 128), jnp.float32)
+        lax.fori_loop(0, count, body, 0)
+
+    steps(2, range(8))
+    steps(2, range(7))
+    steps(1, range(1, 7))
+    mean = jnp.zeros((48, 128), jnp.float32)
+    wide = lanes((16, 128))
     for m in range(3):
-        col = STARTS[m] + lax.broadcasted_iota(jnp.int32, (128, 128), 0)
-        chosen = ((jnp.maximum(col, 0) * 6554) >> 16) == lanes((128, 128))
-        chosen = chosen & (col >= TAKEN[m]) & (col < TAKEN[m + 1])
-        pick = jnp.where(chosen, 1.0, 0.0)
-        mean = mean + jnp.dot(
-            sums[m], pick, precision=lax.Precision.HIGHEST, preferred_element_type=jnp.float32
-        )
+        for l in range(LEV):
+            total = c[0, l, m, pl.ds(18, 4, stride=10), :]
+            for k in range(1, RATIO):
+                total = total + c[0, l, m, pl.ds(18 + k, 4, stride=10), :]
+            sums[m, 4 * l : 4 * l + 4, :] = total
+        taken = (wide >= TAKEN[m] - STARTS[m]) & (wide < TAKEN[m + 1] - STARTS[m])
+        value = jnp.where(taken, sums[m], 0.0)
+        high = value.astype(jnp.bfloat16)
+        value = value - high.astype(jnp.float32)
+        middle = value.astype(jnp.bfloat16)
+        low = (value - middle.astype(jnp.float32)).astype(jnp.bfloat16)
+        away = lax.broadcasted_iota(jnp.int32, (128, 128), 0) + STARTS[m] - RATIO * lanes((128, 128))
+        pick = jnp.where((away >= 0) & (away < RATIO), 1.0, 0.0).astype(jnp.bfloat16)
+        parts = jnp.concatenate([high, middle, low], axis=0)
+        mean = mean + jnp.dot(parts, pick, preferred_element_type=jnp.float32)
+    mean = mean[0:16] + (mean[16:32] + mean[32:48])
     mean = mean * (1.0 / (RATIO * RATIO))
     lane4 = lanes((4, 128))
     value = jnp.zeros((4, 128), jnp.float32)
@@ -305,11 +318,20 @@
         value = jnp.where(inside, turned[l][4 * l : 4 * l + 4, :], value)
     tile_a = lax.div(left[g], COLS)
     tile_b = jnp.where(tile_a < TILES - 1, tile_a + 1, tile_a - 1)
-    back[TILES * src + tile_a] = value
-    back[TILES * src + tile_b] = value
-
-
-def finish_kernel(got_tile, got_grp, c, so2, east, north, diff, stepped, fine_out, px, vk, ed, sems):
+    slot[...] = value
+    stores = [
+        pltpu.make_async_copy(slot, back.at[TILES * src + tile], sems.at[1 + k])
+        for k, tile in enumerate((tile_a, tile_b))
+    ]
+    for store in stores:
+        store.start()
+    for store in stores:
+        store.wait()
+
+
+def finish_kernel(
+    rows, offs, got_tile, got_grp, c, so2, east, north, diff, stepped, fine_out, keep, px, vk, side, sems
+):
     t = lax.axis_index("tile")
     g = lax.axis_index("grp")
     prev_t = jnp.maximum(t - 1, 0)
@@ -328,21 +350,28 @@
     lane = lanes((8, 128))
     wide = lanes((OWN, 128))
     for l in range(LEV):
-        turned = [pltpu.roll(c[0, l, m, 18:58, :], by, 1) for m, by in enumerate((127, 107, 87))]
-        fine_out[0, l, :, 0:128] = jnp.where(wide < 117, turned[0], turned[1])
-        fine_out[0, l, :, 128:256] = jnp.where(wide < 97, turned[1], turned[2])
-        fine_out[0, l, :, 256:320] = turned[2][:, 0:64]
+        middle = pltpu.roll(c[0, l, 1, 18:58, :], 96, 1)
+        last = pltpu.roll(c[0, l, 2, 18:58, :], 64, 1)
+        fine_out[0, l, :, 0:128] = jnp.where(wide < 117, c[0, l, 0, 18:58, :], middle)
+        fine_out[0, l, :, 128:256] = jnp.where(wide < 75, middle, last)
+        fine_out[0, l, :, 256:320] = last[:, 0:64]
     for copy in copies:
         copy.wait()
     for p in range(8):
         px[p, 7:8, :] = jnp.where(g > 0, got_grp[prev_g, WIN + p : WIN + p + 1, :], 0.0)
         px[p, 72:73, :] = jnp.where(g < GROUPS - 1, got_grp[next_g, WIN + p : WIN + p + 1, :], 0.0)
-    for k, tile in enumerate((prev_t, next_t)):
-        packed = got_tile[tile, WIN : WIN + 8, :]
-        ed[k, 0:4, :] = packed[0:4]
-        ed[k, 4:8, :] = pltpu.roll(packed, 64, 1)[0:4]
-    edge_l = jnp.where(t > 0, ed[0], 0.0)
-    edge_r = jnp.where(t < TILES - 1, ed[1], 0.0)
+    here = lax.broadcasted_iota(jnp.int32, (8, 128), 0) == 0
+    for k, (tile, there, at) in enumerate(((prev_t, t > 0, 0), (next_t, t < TILES - 1, 127))):
+        put = jnp.where(here & (lane == at), 1.0, 0.0)
+        for p in range(4):
+            row = jnp.where(there, got_tile[tile, WIN + p : WIN + p + 1, :], 0.0)
+            side[k, 128 * p : 128 * p + 128, :] = lax.dot_general(
+                jnp.broadcast_to(row, (8, 128)),
+                put,
+                (((0,), (0,)), ((), ())),
+                precision=lax.Precision.HIGHEST,
+                preferred_element_type=jnp.float32,
+            )
     for b in range(8):
         r = 8 + 8 * b
         q = slice(8 * b, 8 * b + 8)
@@ -351,12 +380,12 @@
         between = [0.5 * (ks[l] + ks[l + 1]) * (now[l + 1] - now[l]) for l in range(LEV - 1)]
         for l in range(LEV):
             here = now[l]
-            k, kv = 8 * l + b, 32 + 8 * l + b
+            at, vat = 64 * l + 8 * b, 256 + 64 * l + 8 * b
             wind = vk[l, q, :]
-            c_w = jnp.where(lane == 0, pltpu.roll(edge_l, (128 - k) % 128, 1), pltpu.roll(here, 1, 1))
-            c_e = jnp.where(lane == 127, pltpu.roll(edge_r, 127 - k, 1), pltpu.roll(here, 127, 1))
-            v_w = jnp.where(lane == 0, pltpu.roll(edge_l, 128 - kv, 1), pltpu.roll(wind, 1, 1))
-            v_e = jnp.where(lane == 127, pltpu.roll(edge_r, 127 - kv, 1), pltpu.roll(wind, 127, 1))
+            c_w = jnp.where(lane == 0, side[0, at : at + 8, :], pltpu.roll(here, 1, 1))
+            c_e = jnp.where(lane == 127, side[1, at : at + 8, :], pltpu.roll(here, 127, 1))
+            v_w = jnp.where(lane == 0, side[0, vat : vat + 8, :], pltpu.roll(wind, 1, 1))
+            v_e = jnp.where(lane == 127, side[1, vat : vat + 8, :], pltpu.roll(wind, 127, 1))
             c_n = px[l, r - 1 : r + 7, :]
             c_s = px[l, r + 1 : r + 9, :]
             flow = px[4 + l, r : r + 8, :]
@@ -375,9 +404,13 @@
             if l > 0:
                 value = value - between[l - 1]
             stepped[l, q, :] = value
-
-
-def place_kernel(rows, offs, left, height, width, stepped, got, out, s, sems):
+    off = offs[nest_over(rows, g)]
+    base = pl.multiple_of(lax.div(off, 8) * 8, 8)
+    for l in range(LEV):
+        keep[l] = stepped[l, pl.ds(base, 40), :]
+
+
+def place_kernel(rows, offs, left, height, width, stepped, keep, got, out, s, sems):
     t = lax.axis_index("tile")
     g = lax.axis_index("grp")
     n = nest_over(rows, g)
@@ -388,17 +421,15 @@
     def _():
         off = offs[n]
         base = pl.multiple_of(lax.div(off, 8) * 8, 8)
-        load_s = pltpu.make_async_copy(stepped.at[:, pl.ds(base, 40), :], s, sems.at[0])
-        load_s.start()
         lane = lanes((FR, 128)) + COLS * t
         row = lax.broadcasted_iota(jnp.int32, (FR, 128), 0)
         covered = (lane >= lf) & (lane < lf + wd) & (row < height[n])
-        load_s.wait()
+        at = pl.ds(off - base, FR)
         for l in range(LEV):
             turned = pltpu.roll(got[n], lax.rem(lf - COLS * t - 32 * l + 2048, 128), 1)
-            at = pl.ds(off - base, FR)
-            s[l, at, :] = jnp.where(covered, turned, s[l, at, :])
-        store = pltpu.make_async_copy(s, out.at[:, pl.ds(base, 40), :], sems.at[1])
+            s[l] = keep[l]
+            s[l, at, :] = jnp.where(covered, turned, keep[l, at, :])
+        store = pltpu.make_async_copy(s, out.at[:, pl.ds(base, 40), :], sems.at[0])
         store.start()
         store.wait()
 
@@ -414,7 +445,12 @@
         out_shape=(field((TILES, SLOT, 128)), field((16, 128))),
         in_specs=[SMEM] * 3 + [ANY] * 5,
         out_specs=(VMEM, VMEM),
-        scratch_shapes=[field((16, ROWS + 8, 128)), field((LEV, OWN, WIDE)), dma((5,))],
+        scratch_shapes=[
+            field((16, ROWS + 8, 128)),
+            field((LEV, OWN, WIDE)),
+            field((5, 40, 128)),
+            dma((5,)),
+        ],
         name="pack",
     )(rows, offs, left, so2, east, north, diff, nest)
     got_tile = near(lax.all_to_all(send, "tile", 0, 0))
@@ -428,10 +464,11 @@
     got_grp = near(lax.all_to_all(send, "grp", 0, 0))
     c, back = pl.pallas_call(
         fine_kernel,
-        out_shape=(field((2, LEV, 3, 80, 128)), field((GROUPS * TILES, 4, 128))),
+        out_shape=(field((2, LEV, 3, 80, 128)), shape((GROUPS * TILES, 4, 128), f32)),
         in_specs=[SMEM] * 4 + [VMEM] * 2 + [ANY],
-        out_specs=(VMEM, VMEM),
+        out_specs=(VMEM, ANY),
         scratch_shapes=[
+            field((4, 128)),
             field((LEV, OWN, WIDE)),
             field((LEV, OWN, 128)),
             field((11 * LEV - 1, 3, 8, 128)),
@@ -443,34 +480,38 @@
             field((LEV, 3, 64, 128)),
             field((LEV - 1, 3, 64, 128)),
             field((3, 16, 128)),
-            dma((1,)),
+            dma((3,)),
         ],
         name="fine",
     )(rows, left, height, width, got_tile, got_grp, nest)
-    stepped, nest_next = pl.pallas_call(
+    stepped, nest_next, keep = pl.pallas_call(
         finish_kernel,
-        out_shape=(shape((LEV, ROWS, COLS), f32), shape((1, LEV, OWN, WIDE), f32)),
-        in_specs=[VMEM] * 3 + [ANY] * 4,
-        out_specs=(VMEM, VMEM),
+        out_shape=(
+            shape((LEV, ROWS, COLS), f32),
+            shape((1, LEV, OWN, WIDE), f32),
+            field((LEV, 40, 128)),
+        ),
+        in_specs=[SMEM] * 2 + [VMEM] * 3 + [ANY] * 4,
+        out_specs=(VMEM, VMEM, VMEM),
         scratch_shapes=[
             field((8, ROWS + 16, 128)),
             field((8, ROWS, 128)),
-            field((2, 8, 128)),
+            field((2, 512, 128)),
             dma((4,)),
         ],
         name="finish",
-    )(got_tile, got_grp, near(c), so2, east, north, diff)
+    )(rows, offs, got_tile, got_grp, near(c), so2, east, north, diff)
     got = lax.all_to_all(back, ("grp", "tile"), 0, 0)
     got = near(got.reshape(GROUPS, FR, 128))
     parent_next = pl.pallas_call(
         place_kernel,
         out_shape=shape((LEV, ROWS, COLS), f32),
-        in_specs=[SMEM] * 5 + [ANY, VMEM],
+        in_specs=[SMEM] * 5 + [ANY, VMEM, VMEM],
         out_specs=ANY,
-        scratch_shapes=[field((LEV, 40, 128)), dma((2,))],
+        scratch_shapes=[field((LEV, 40, 128)), dma((1,))],
         input_output_aliases={5: 0},
         name="place",
-    )(rows, offs, left, height, width, stepped, got)
+    )(rows, offs, left, height, width, stepped, near(keep), got)
     return parent_next, nest_next
 
 

time: 61.8 us -> 58.9 us (0.953); the launches traced: 62.3 us -> 58.5 us
  Pallas kernels: 14.8 us -> 12 us
  waiting for transfers between devices: 9.09 us -> 8.17 us
    pallas_call x1, Pallas kernels: 7.06 us -> 5.01 us  [shards(): pl.pallas_call(fine_kernel, out_shape=(field((2, LEV, 3, 80, 128)), shape...]
    pallas_call x1, Pallas kernels: 2.35 us -> 0.74 us  [shards(): pl.pallas_call(place_kernel, out_shape=shape((LEV, ROWS, COLS), f32), in_...]
    pallas_call x1, Pallas kernels: 2.24 us -> 3.16 us  [shards(): pl.pallas_call(finish_kernel, out_shape=(shape((LEV, ROWS, COLS), f32), s...]
    all_to_all x1, waiting for transfers between devices: 9.09 us -> 8.17 us  [shards(): got = lax.all_to_all(back, ('grp', 'tile'), 0, 0)]
  transfers between devices with their start and end apart: 1 -> 1, of which waited for: 1 -> 1; matrix products, arithmetic and copies ran while one was open for 0% -> 0% of each run, Pallas kernels for 4% -> 5%
where the time goes in v2:
time: 58.9 us; the launch traced here: 58.5 us
  blocking collectives  33.8 us (57%)
  Pallas kernels  12 us (20%)
  waiting for transfers between devices  8.17 us (14%)
  starting transfers between devices  3.92 us (7%)
  between operations  0.67 us (1%)
    all_to_all x1, blocking collectives, shards(): got_tile = near(lax.all_to_all(send, 'tile', 0, 0))  18.9 us
    all_to_all x1, blocking collectives, shards(): got_grp = near(lax.all_to_all(send, 'grp', 0, 0))  14.9 us
    all_to_all x1, waiting for transfers between devices, shards(): got = lax.all_to_all(back, ('grp', 'tile'), 0, 0)  8.17 us
    pallas_call x1, Pallas kernels, shards(): pl.pallas_call(fine_kernel, out_shape=(field((2, LEV, 3, 80, 128)), shape...  5.01 us
    all_to_all x1, starting transfers between devices, shards(): got = lax.all_to_all(back, ('grp', 'tile'), 0, 0)  3.92 us
    pallas_call x1, Pallas kernels, shards(): pl.pallas_call(finish_kernel, out_shape=(shape((LEV, ROWS, COLS), f32), s...  3.16 us
    pallas_call x1, Pallas kernels, shards(): pl.pallas_call(pack_kernel, out_shape=(field((TILES, SLOT, 128)), field((...  2.37 us
  transfers between devices with their start and end apart: 1, of which 1 were waited for; matrix products, arithmetic and copies ran while one was open for 0% of the time, Pallas kernels for 5%

profile of v2, /device:TPU:1, one launch (start us, length us, event | category | flops | bytes accessed | tf_op | source)
XLA Modules:
  0.0 58.5 jit_solution(12666462296314801601)
XLA Ops:
  0.6 2.4 %pack.1 = (f32[8,136,128]{2,1,0:T(8,128)S(1)}, f32[16,128]{1,0:T(8,128)S(1)}) custom-call(s32[16]{0:T(128)} %rows.9, s32[16]{0:T(128)} %offs.5, s32[16]{0:T(128)} %left.7, f32[4,64,128]{2,1,0:T(8,128)} %so2.3, f32[4,64,128]{2,1,0:T(8,128)} %east.3, f32[4,64,128]{2,1,0:T(8,128)} %north.3, f32[4,64,128]{2,1,0:T(8,128)} %diff.3, f32[1,4,40,320]{3,2,1,0:T(8,128)} %nest.3), custom_call_target="tpu_custom_call" | custom-call | tf_op jit(solution)/shard_map/pack/pallas_call | solution.py:443
  3.0 18.9 %all_to_all.15.got.got_tile = f32[8,136,128]{2,1,0:T(8,128)S(1)} all-to-all(f32[8,136,128]{2,1,0:T(8,128)S(1)} %get-tuple-element.9), channel_id=1, replica_groups=mesh['grp'=16,'tile'=8] {'tile'}, dimensions={0} | all-to-all | bytes 1114112 | tf_op jit(solution)/shard_map/all_to_all | solution.py:456
  21.9 0.7 %merge.1 = f32[16,40,128]{2,1,0:T(8,128)S(1)} custom-call(s32[16]{0:T(128)} %rows.9, s32[16]{0:T(128)} %left.7, f32[8,136,128]{2,1,0:T(8,128)S(1)} %all_to_all.15.got.got_tile, f32[16,128]{1,0:T(8,128)S(1)} %get-tuple-element.10.edges), custom_call_target="tpu_custom_call" | custom-call | tf_op jit(solution)/shard_map/merge/pallas_call | solution.py:457
  22.6 14.9 %all_to_all.16.got_grp = f32[16,40,128]{2,1,0:T(8,128)S(1)} all-to-all(f32[16,40,128]{2,1,0:T(8,128)S(1)} %merge.1), channel_id=1, replica_groups=mesh['grp'=16,'tile'=8] {'grp'}, dimensions={0} | all-to-all | bytes 655360 | tf_op jit(solution)/shard_map/all_to_all | solution.py:464
  37.5 5.0 %fine.1 = (f32[2,4,3,80,128]{4,3,2,1,0:T(8,128)S(1)}, f32[128,4,128]{2,1,0:T(4,128)}) custom-call(s32[16]{0:T(128)} %rows.9, s32[16]{0:T(128)} %left.7, s32[16]{0:T(128)} %height.3, s32[16]{0:T(128)} %width.3, f32[8,136,128]{2,1,0:T(8,128)S(1)} %all_to_all.15.got.got_tile, f32[16,40,128]{2,1,0:T(8,128)S(1)} %all_to_all.16.got_grp, f32[1,4,40,320]{3,2,1,0:T(8,128)} %nest.3), custom_call_target="tpu_custom_call" | custom-call | tf_op jit(solution)/shard_map/fine/pallas_call | solution.py:465
  42.5 3.9 %all-to-all-start.2 = ((f32[128,4,128]{2,1,0:T(4,128)}), f32[128,4,128]{2,1,0:T(4,128)S(1)}, u32[]{:S(2)}, u32[]{:S(2)}) async-start(f32[128,4,128]{2,1,0:T(4,128)} %get-tuple-element.14), calls=%async_computation.2 | async-start | bytes 524288 | tf_op jit(solution)/shard_map/all_to_all | solution.py:504
  46.5 3.2 %finish.1 = (f32[4,64,128]{2,1,0:T(8,128)}, f32[1,4,40,320]{3,2,1,0:T(8,128)}, f32[4,40,128]{2,1,0:T(8,128)S(1)}) custom-call(s32[16]{0:T(128)} %rows.9, s32[16]{0:T(128)} %offs.5, f32[8,136,128]{2,1,0:T(8,128)S(1)} %all_to_all.15.got.got_tile, f32[16,40,128]{2,1,0:T(8,128)S(1)} %all_to_all.16.got_grp, f32[2,4,3,80,128]{4,3,2,1,0:T(8,128)S(1)} %get-tuple-element.11.c, ...), custom_call_target="tpu_custom_call" | custom-call | tf_op jit(solution)/shard_map/finish/pallas_call | solution.py:487
  49.6 8.2 %all-to-all-done.2 = f32[128,4,128]{2,1,0:T(4,128)S(1)} async-done(((f32[128,4,128]{2,1,0:T(4,128)}), f32[128,4,128]{2,1,0:T(4,128)S(1)}, u32[]{:S(2)}, u32[]{:S(2)}) %all-to-all-start.2) | async-done | bytes 262176 | tf_op jit(solution)/shard_map/all_to_all | solution.py:504
  57.8 0.7 %place.1 = f32[4,64,128]{2,1,0:T(8,128)} custom-call(s32[16]{0:T(128)} %rows.9, s32[16]{0:T(128)} %offs.5, s32[16]{0:T(128)} %left.7, s32[16]{0:T(128)} %height.3, s32[16]{0:T(128)} %width.3, f32[4,64,128]{2,1,0:T(8,128)} %get-tuple-element.12.stepped, f32[4,40,128]{2,1,0:T(8,128)S(1)} %get-tuple-element.13.keep, ...), custom_call_target="tpu_custom_call", output_to_operand_aliasing={{}: (5, {})} | custom-call | tf_op jit(solution)/shard_map/place/pallas_call | solution.py:506
Async XLA Ops:
  42.5 15.3 %all-to-all-start.2 = ((f32[128,4,128]{2,1,0:T(4,128)}), f32[128,4,128]{2,1,0:T(4,128)S(1)}, u32[]{:S(2)}, u32[]{:S(2)}) async-start(f32[128,4,128]{2,1,0:T(4,128)} %get-tuple-element.14), calls=%async_computation.2 | async-start | bytes 524288 | tf_op jit(solution)/shard_map/all_to_all | solution.py:504

commit v3 on v2

--- a/solution.py
+++ b/solution.py
@@ -40,7 +40,9 @@
     return lax.broadcasted_iota(jnp.int32, shape, 1)
 
 
-def pack_kernel(rows, offs, left, so2, east, north, diff, nest, send, edges, x, nx, cut, sems):
+def pack_kernel(
+    rows, offs, left, height, width, so2, east, north, diff, nest, send, edges, facts, x, nx, cut, sems
+):
     t = lax.axis_index("tile")
     g = lax.axis_index("grp")
     loads = [
@@ -51,6 +53,15 @@
     for c in loads:
         c.start()
     n = nest_over(rows, g)
+    facts[0] = n
+    facts[1] = left[n]
+    facts[2] = offs[n]
+    facts[3] = height[n]
+    facts[4] = width[n]
+    facts[5] = rows[g]
+    facts[6] = left[g]
+    facts[7] = height[g]
+    facts[8] = width[g]
     top = offs[n] - 1
     base = 128 * t + 1 - left[n] + 1024
     x[:, ROWS : ROWS + 8, :] = jnp.zeros((16, 8, 128), jnp.float32)
@@ -104,10 +115,10 @@
             send[d, WIN + k : WIN + k + 1, :] = jnp.where(d < t, pair[0:1], pair[1:2])
 
 
-def merge_kernel(rows, left, got, edges, send):
+def merge_kernel(facts, got, edges, send):
     g = lax.axis_index("grp")
-    n = nest_over(rows, g)
-    start = left[n] - 1
+    n = facts[0]
+    start = facts[1] - 1
     first = lax.div(start, COLS)
     second = jnp.minimum(first + 1, TILES - 1)
     send[jnp.where(g > 0, g - 1, g + 2), WIN : WIN + 8, :] = edges[0:8, :]
@@ -141,13 +152,13 @@
 
 
 def fine_kernel(
-    rows, left, height, width, got_tile, got_grp, nest,
+    facts, got_tile, got_grp, nest,
     c, back,
     slot, nx, last_part, e, raw, am, ap, bm, bp, ac, kz, sums, sems,
 ):
     t = lax.axis_index("tile")
     g = lax.axis_index("grp")
-    src = rows[g]
+    src = facts[5]
     prev_t = jnp.maximum(t - 1, 0)
     next_t = jnp.minimum(t + 1, TILES - 1)
     load = pltpu.make_async_copy(nest.at[0], nx, sems.at[0])
@@ -163,14 +174,14 @@
                 c[p, l, m, 72:80, :] = zero
 
     above = OWN // RATIO * t - 1 + sub
-    row_in = (above >= 0) & (above < height[g])
+    row_in = (above >= 0) & (above < facts[7])
     coarse = {}
     for m in range(3):
         col = columns(m, lane)
         under = (jnp.maximum(col, 0) * 6554) >> 16
         pick = jnp.where(col < 0, 0, jnp.where(col < WIDE, under + 1, SPAN - 1))
         kpick = jnp.minimum(under, FR - 1)
-        inside = row_in & (col >= 0) & (col < RATIO * width[g])
+        inside = row_in & (col >= 0) & (col < RATIO * facts[8])
         block = got_grp[src, 24:32, :]
         ks = [jnp.take_along_axis(block, kpick + 32 * l, axis=1) for l in range(LEV)]
         faces = [0.05 * (ks[l] + ks[l + 1]) for l in range(LEV - 1)]
@@ -248,7 +259,7 @@
         for tile, at in ((prev_t, 0), (next_t, OWN + 10)):
             spots = (EDGE + 20 * l, EDGE + 20 * l + 10, EDGE + 80 + 10 * (l // 2))
             lay(l, at, 10, [got_tile[tile, k : k + 10, :] for k in spots], l % 2 == 0)
-    last_row = RATIO * height[g]
+    last_row = RATIO * facts[7]
     first_row = OWN * t - 10
     for i in range(8):
         r = 8 + 8 * i
@@ -256,7 +267,7 @@
         row_in = (row >= 0) & (row < last_row)
         for m in range(3):
             col = columns(m, lane)
-            active = row_in & (col >= 0) & (col < RATIO * width[g])
+            active = row_in & (col >= 0) & (col < RATIO * facts[8])
             for l in range(LEV):
                 c[0, l, m, r : r + 8, :] = jnp.where(active, raw[l, m, r - 8 : r, :], spread(l, m, i))
 
@@ -316,7 +327,7 @@
     for l in range(LEV):
         inside = (lane4 >= 32 * l) & (lane4 < 32 * l + 32)
         value = jnp.where(inside, turned[l][4 * l : 4 * l + 4, :], value)
-    tile_a = lax.div(left[g], COLS)
+    tile_a = lax.div(facts[6], COLS)
     tile_b = jnp.where(tile_a < TILES - 1, tile_a + 1, tile_a - 1)
     slot[...] = value
     stores = [
@@ -330,7 +341,7 @@
 
 
 def finish_kernel(
-    rows, offs, got_tile, got_grp, c, so2, east, north, diff, stepped, fine_out, keep, px, vk, side, sems
+    facts, got_tile, got_grp, c, so2, east, north, diff, stepped, fine_out, keep, px, vk, side, sems
 ):
     t = lax.axis_index("tile")
     g = lax.axis_index("grp")
@@ -404,26 +415,23 @@
             if l > 0:
                 value = value - between[l - 1]
             stepped[l, q, :] = value
-    off = offs[nest_over(rows, g)]
+    off = facts[2]
     base = pl.multiple_of(lax.div(off, 8) * 8, 8)
     for l in range(LEV):
         keep[l] = stepped[l, pl.ds(base, 40), :]
 
 
-def place_kernel(rows, offs, left, height, width, stepped, keep, got, out, s, sems):
+def place_kernel(facts, stepped, keep, got, out, s, sems):
     t = lax.axis_index("tile")
-    g = lax.axis_index("grp")
-    n = nest_over(rows, g)
-    lf = left[n]
-    wd = width[n]
+    n, lf, wd = facts[0], facts[1], facts[4]
 
     @pl.when((lf < COLS * t + COLS) & (lf + wd > COLS * t))
     def _():
-        off = offs[n]
+        off = facts[2]
         base = pl.multiple_of(lax.div(off, 8) * 8, 8)
         lane = lanes((FR, 128)) + COLS * t
         row = lax.broadcasted_iota(jnp.int32, (FR, 128), 0)
-        covered = (lane >= lf) & (lane < lf + wd) & (row < height[n])
+        covered = (lane >= lf) & (lane < lf + wd) & (row < facts[3])
         at = pl.ds(off - base, FR)
         for l in range(LEV):
             turned = pltpu.roll(got[n], lax.rem(lf - COLS * t - 32 * l + 2048, 128), 1)
@@ -440,11 +448,16 @@
     dma = pltpu.SemaphoreType.DMA
     field = functools.partial(pltpu.VMEM, dtype=f32)
     near = functools.partial(pltpu.with_memory_space_constraint, memory_space=pltpu.VMEM)
-    send, edges = pl.pallas_call(
+    scalar = functools.partial(pltpu.with_memory_space_constraint, memory_space=pltpu.SMEM)
+    send, edges, facts = pl.pallas_call(
         pack_kernel,
-        out_shape=(field((TILES, SLOT, 128)), field((16, 128))),
-        in_specs=[SMEM] * 3 + [ANY] * 5,
-        out_specs=(VMEM, VMEM),
+        out_shape=(
+            field((TILES, SLOT, 128)),
+            field((16, 128)),
+            pltpu.SMEM((16,), jnp.int32),
+        ),
+        in_specs=[SMEM] * 5 + [ANY] * 5,
+        out_specs=(VMEM, VMEM, SMEM),
         scratch_shapes=[
             field((16, ROWS + 8, 128)),
             field((LEV, OWN, WIDE)),
@@ -452,20 +465,21 @@
             dma((5,)),
         ],
         name="pack",
-    )(rows, offs, left, so2, east, north, diff, nest)
+    )(rows, offs, left, height, width, so2, east, north, diff, nest)
+    facts = scalar(facts)
     got_tile = near(lax.all_to_all(send, "tile", 0, 0))
     send = pl.pallas_call(
         merge_kernel,
         out_shape=field((GROUPS, GSLOT, 128)),
-        in_specs=[SMEM] * 2 + [VMEM, VMEM],
+        in_specs=[SMEM, VMEM, VMEM],
         out_specs=VMEM,
         name="merge",
-    )(rows, left, got_tile, near(edges))
+    )(facts, got_tile, near(edges))
     got_grp = near(lax.all_to_all(send, "grp", 0, 0))
     c, back = pl.pallas_call(
         fine_kernel,
         out_shape=(field((2, LEV, 3, 80, 128)), shape((GROUPS * TILES, 4, 128), f32)),
-        in_specs=[SMEM] * 4 + [VMEM] * 2 + [ANY],
+        in_specs=[SMEM] + [VMEM] * 2 + [ANY],
         out_specs=(VMEM, ANY),
         scratch_shapes=[
             field((4, 128)),
@@ -483,7 +497,7 @@
             dma((3,)),
         ],
         name="fine",
-    )(rows, left, height, width, got_tile, got_grp, nest)
+    )(facts, got_tile, got_grp, nest)
     stepped, nest_next, keep = pl.pallas_call(
         finish_kernel,
         out_shape=(
@@ -491,7 +505,7 @@
             shape((1, LEV, OWN, WIDE), f32),
             field((LEV, 40, 128)),
         ),
-        in_specs=[SMEM] * 2 + [VMEM] * 3 + [ANY] * 4,
+        in_specs=[SMEM] + [VMEM] * 3 + [ANY] * 4,
         out_specs=(VMEM, VMEM, VMEM),
         scratch_shapes=[
             field((8, ROWS + 16, 128)),
@@ -500,18 +514,18 @@
             dma((4,)),
         ],
         name="finish",
-    )(rows, offs, got_tile, got_grp, near(c), so2, east, north, diff)
+    )(facts, got_tile, got_grp, near(c), so2, east, north, diff)
     got = lax.all_to_all(back, ("grp", "tile"), 0, 0)
     got = near(got.reshape(GROUPS, FR, 128))
     parent_next = pl.pallas_call(
         place_kernel,
         out_shape=shape((LEV, ROWS, COLS), f32),
-        in_specs=[SMEM] * 5 + [ANY, VMEM, VMEM],
+        in_specs=[SMEM, ANY, VMEM, VMEM],
         out_specs=ANY,
         scratch_shapes=[field((LEV, 40, 128)), dma((1,))],
-        input_output_aliases={5: 0},
+        input_output_aliases={1: 0},
         name="place",
-    )(rows, offs, left, height, width, stepped, near(keep), got)
+    )(facts, stepped, near(keep), got)
     return parent_next, nest_next
 
 

time: 58.9 us -> 56.8 us (0.964)
  Pallas kernels: 12 us -> 9.23 us
  waiting for transfers between devices: 8.17 us -> 8.83 us
    pallas_call x1, Pallas kernels: 0.74 us -> 0.01 us  [shards(): pl.pallas_call(place_kernel, out_shape=shape((LEV, ROWS, COLS), f32), in_...]
    pallas_call x1, Pallas kernels: 0.71 us -> 0.01 us  [shards(): pl.pallas_call(merge_kernel, out_shape=field((GROUPS, GSLOT, 128)), in_sp...]
    pallas_call x1, Pallas kernels: 5.01 us -> 4.33 us  [shards(): pl.pallas_call(fine_kernel, out_shape=(field((2, LEV, 3, 80, 128)), shape...]
    pallas_call x1, Pallas kernels: 3.16 us -> 2.5 us  [shards(): pl.pallas_call(finish_kernel, out_shape=(shape((LEV, ROWS, COLS), f32), s...]
    all_to_all x1, waiting for transfers between devices: 8.17 us -> 8.83 us  [shards(): got = lax.all_to_all(back, ('grp', 'tile'), 0, 0)]
  transfers between devices with their start and end apart: 1 -> 1, of which waited for: 1 -> 1; matrix products, arithmetic and copies ran while one was open for 0% -> 0% of each run, Pallas kernels for 5% -> 4%
where the time goes in v3:
time: 56.8 us; the launch traced here: 56.4 us
  blocking collectives  33.8 us (60%)
  Pallas kernels  9.23 us (16%)
  waiting for transfers between devices  8.83 us (16%)
  starting transfers between devices  3.91 us (7%)
  between operations  0.67 us (1%)
    all_to_all x1, blocking collectives, shards(): got_tile = near(lax.all_to_all(send, 'tile', 0, 0))  18.9 us
    all_to_all x1, blocking collectives, shards(): got_grp = near(lax.all_to_all(send, 'grp', 0, 0))  14.9 us
    all_to_all x1, waiting for transfers between devices, shards(): got = lax.all_to_all(back, ('grp', 'tile'), 0, 0)  8.83 us
    pallas_call x1, Pallas kernels, shards(): pl.pallas_call(fine_kernel, out_shape=(field((2, LEV, 3, 80, 128)), shape...  4.33 us
    all_to_all x1, starting transfers between devices, shards(): got = lax.all_to_all(back, ('grp', 'tile'), 0, 0)  3.91 us
    pallas_call x1, Pallas kernels, shards(): pl.pallas_call(finish_kernel, out_shape=(shape((LEV, ROWS, COLS), f32), s...  2.5 us
    pallas_call x1, Pallas kernels, shards(): pl.pallas_call(pack_kernel, out_shape=(field((TILES, SLOT, 128)), field((...  2.39 us
  transfers between devices with their start and end apart: 1, of which 1 were waited for; matrix products, arithmetic and copies ran while one was open for 0% of the time, Pallas kernels for 4%

profile of v3, /device:TPU:1, one launch (start us, length us, event | category | flops | bytes accessed | tf_op | source)
XLA Modules:
  0.0 56.4 jit_solution(10542799955992693347)
XLA Ops:
  0.6 2.4 %pack.1 = (f32[8,136,128]{2,1,0:T(8,128)S(1)}, f32[16,128]{1,0:T(8,128)S(1)}, s32[16]{0:T(128)S(4)}) custom-call(s32[16]{0:T(128)} %rows.1, s32[16]{0:T(128)} %offs.1, s32[16]{0:T(128)} %left.1, s32[16]{0:T(128)} %height.1, s32[16]{0:T(128)} %width.1, f32[4,64,128]{2,1,0:T(8,128)} %so2.3, f32[4,64,128]{2,1,0:T(8,128)} %east.3, f32[4,64,128]{2,1,0:T(8,128)} %north.3, ...), custom_call_target="tpu_custom_call" | custom-call | tf_op jit(solution)/shard_map/pack/pallas_call | solution.py:452
  3.0 18.9 %all_to_all.15.got.got_tile = f32[8,136,128]{2,1,0:T(8,128)S(1)} all-to-all(f32[8,136,128]{2,1,0:T(8,128)S(1)} %get-tuple-element.11), channel_id=1, replica_groups=mesh['grp'=16,'tile'=8] {'tile'}, dimensions={0} | all-to-all | bytes 1114112 | tf_op jit(solution)/shard_map/all_to_all | solution.py:470
  22.0 14.9 %all_to_all.16.got_grp = f32[16,40,128]{2,1,0:T(8,128)S(1)} all-to-all(f32[16,40,128]{2,1,0:T(8,128)S(1)} %merge.1), channel_id=1, replica_groups=mesh['grp'=16,'tile'=8] {'grp'}, dimensions={0} | all-to-all | bytes 655360 | tf_op jit(solution)/shard_map/all_to_all | solution.py:478
  36.8 4.3 %fine.1 = (f32[2,4,3,80,128]{4,3,2,1,0:T(8,128)S(1)}, f32[128,4,128]{2,1,0:T(4,128)}) custom-call(s32[16]{0:T(128)S(4)} %get-tuple-element.10.facts, f32[8,136,128]{2,1,0:T(8,128)S(1)} %all_to_all.15.got.got_tile, f32[16,40,128]{2,1,0:T(8,128)S(1)} %all_to_all.16.got_grp, f32[1,4,40,320]{3,2,1,0:T(8,128)} %nest.3), custom_call_target="tpu_custom_call" | custom-call | tf_op jit(solution)/shard_map/fine/pallas_call | solution.py:479
  41.2 3.9 %all-to-all-start.2 = ((f32[128,4,128]{2,1,0:T(4,128)}), f32[128,4,128]{2,1,0:T(4,128)S(1)}, u32[]{:S(2)}, u32[]{:S(2)}) async-start(f32[128,4,128]{2,1,0:T(4,128)} %get-tuple-element.16), calls=%async_computation.2 | async-start | bytes 524288 | tf_op jit(solution)/shard_map/all_to_all | solution.py:518
  45.1 2.5 %finish.1 = (f32[4,64,128]{2,1,0:T(8,128)}, f32[1,4,40,320]{3,2,1,0:T(8,128)}, f32[4,40,128]{2,1,0:T(8,128)S(1)}) custom-call(s32[16]{0:T(128)S(4)} %get-tuple-element.10.facts, f32[8,136,128]{2,1,0:T(8,128)S(1)} %all_to_all.15.got.got_tile, f32[16,40,128]{2,1,0:T(8,128)S(1)} %all_to_all.16.got_grp, f32[2,4,3,80,128]{4,3,2,1,0:T(8,128)S(1)} %get-tuple-element.13.c, ...), custom_call_target="tpu_custom_call" | custom-call | tf_op jit(solution)/shard_map/finish/pallas_call | solution.py:501
  47.6 8.8 %all-to-all-done.2 = f32[128,4,128]{2,1,0:T(4,128)S(1)} async-done(((f32[128,4,128]{2,1,0:T(4,128)}), f32[128,4,128]{2,1,0:T(4,128)S(1)}, u32[]{:S(2)}, u32[]{:S(2)}) %all-to-all-start.2) | async-done | bytes 262176 | tf_op jit(solution)/shard_map/all_to_all | solution.py:518
  (2 shorter events, 0.0 us)
Async XLA Ops:
  41.2 15.2 %all-to-all-start.2 = ((f32[128,4,128]{2,1,0:T(4,128)}), f32[128,4,128]{2,1,0:T(4,128)S(1)}, u32[]{:S(2)}, u32[]{:S(2)}) async-start(f32[128,4,128]{2,1,0:T(4,128)} %get-tuple-element.16), calls=%async_computation.2 | async-start | bytes 524288 | tf_op jit(solution)/shard_map/all_to_all | solution.py:518

commit v4 on v3

--- a/solution.py
+++ b/solution.py
@@ -41,10 +41,20 @@
 
 
 def pack_kernel(
-    rows, offs, left, height, width, so2, east, north, diff, nest, send, edges, facts, x, nx, cut, sems
+    rows_at, offs_at, left_at, height_at, width_at, so2, east, north, diff, nest,
+    send, edges, facts, nx,
+    rows, offs, left, height, width, x, cut, sems,
 ):
     t = lax.axis_index("tile")
     g = lax.axis_index("grp")
+    numbers = [
+        pltpu.make_async_copy(s, d, sems.at[5 + i])
+        for i, (s, d) in enumerate(
+            ((rows_at, rows), (offs_at, offs), (left_at, left), (height_at, height), (width_at, width))
+        )
+    ]
+    for c in numbers:
+        c.start()
     loads = [
         pltpu.make_async_copy(f, x.at[pl.ds(4 * i, 4), pl.ds(0, ROWS), :], sems.at[i])
         for i, f in enumerate((so2, east, north, diff))
@@ -52,6 +62,8 @@
     loads.append(pltpu.make_async_copy(nest.at[0], nx, sems.at[4]))
     for c in loads:
         c.start()
+    for c in numbers:
+        c.wait()
     n = nest_over(rows, g)
     facts[0] = n
     facts[1] = left[n]
@@ -152,17 +164,15 @@
 
 
 def fine_kernel(
-    facts, got_tile, got_grp, nest,
+    facts, got_tile, got_grp, nx,
     c, back,
-    slot, nx, last_part, e, raw, am, ap, bm, bp, ac, kz, sums, sems,
+    slot, last_part, e, raw, am, ap, bm, bp, ac, kz, sums, sems,
 ):
     t = lax.axis_index("tile")
     g = lax.axis_index("grp")
     src = facts[5]
     prev_t = jnp.maximum(t - 1, 0)
     next_t = jnp.minimum(t + 1, TILES - 1)
-    load = pltpu.make_async_copy(nest.at[0], nx, sems.at[0])
-    load.start()
     lane = lanes((8, 128))
     sub = lax.broadcasted_iota(jnp.int32, (8, 128), 0)
     zero = jnp.zeros((8, 128), jnp.float32)
@@ -243,7 +253,6 @@
                 bm[l, m, q, :] = spread(8 * LEV + l, m, i)
                 bp[l, m, q, :] = spread(9 * LEV + l, m, i)
 
-    load.wait()
 
     def lay(l, at, n, parts, turn):
         wide = lanes((n, 128))
@@ -331,7 +340,7 @@
     tile_b = jnp.where(tile_a < TILES - 1, tile_a + 1, tile_a - 1)
     slot[...] = value
     stores = [
-        pltpu.make_async_copy(slot, back.at[TILES * src + tile], sems.at[1 + k])
+        pltpu.make_async_copy(slot, back.at[TILES * src + tile], sems.at[k])
         for k, tile in enumerate((tile_a, tile_b))
     ]
     for store in stores:
@@ -449,20 +458,21 @@
     field = functools.partial(pltpu.VMEM, dtype=f32)
     near = functools.partial(pltpu.with_memory_space_constraint, memory_space=pltpu.VMEM)
     scalar = functools.partial(pltpu.with_memory_space_constraint, memory_space=pltpu.SMEM)
-    send, edges, facts = pl.pallas_call(
+    send, edges, facts, own = pl.pallas_call(
         pack_kernel,
         out_shape=(
             field((TILES, SLOT, 128)),
             field((16, 128)),
             pltpu.SMEM((16,), jnp.int32),
+            field((LEV, OWN, WIDE)),
         ),
-        in_specs=[SMEM] * 5 + [ANY] * 5,
-        out_specs=(VMEM, VMEM, SMEM),
-        scratch_shapes=[
+        in_specs=[ANY] * 10,
+        out_specs=(VMEM, VMEM, SMEM, VMEM),
+        scratch_shapes=[pltpu.SMEM((16,), jnp.int32)] * 5
+        + [
             field((16, ROWS + 8, 128)),
-            field((LEV, OWN, WIDE)),
             field((5, 40, 128)),
-            dma((5,)),
+            dma((10,)),
         ],
         name="pack",
     )(rows, offs, left, height, width, so2, east, north, diff, nest)
@@ -479,11 +489,10 @@
     c, back = pl.pallas_call(
         fine_kernel,
         out_shape=(field((2, LEV, 3, 80, 128)), shape((GROUPS * TILES, 4, 128), f32)),
-        in_specs=[SMEM] + [VMEM] * 2 + [ANY],
+        in_specs=[SMEM] + [VMEM] * 3,
         out_specs=(VMEM, ANY),
         scratch_shapes=[
             field((4, 128)),
-            field((LEV, OWN, WIDE)),
             field((LEV, OWN, 128)),
             field((11 * LEV - 1, 3, 8, 128)),
             field((LEV, 3, 64, 128)),
@@ -494,10 +503,10 @@
             field((LEV, 3, 64, 128)),
             field((LEV - 1, 3, 64, 128)),
             field((3, 16, 128)),
-            dma((3,)),
+            dma((2,)),
         ],
         name="fine",
-    )(facts, got_tile, got_grp, nest)
+    )(facts, got_tile, got_grp, near(own))
     stepped, nest_next, keep = pl.pallas_call(
         finish_kernel,
         out_shape=(

time: 56.8 us -> 55.9 us (0.984)
  Pallas kernels: 9.23 us -> 8.01 us
    pallas_call x1, Pallas kernels: 2.39 us -> 1.74 us  [shards(): pl.pallas_call(pack_kernel, out_shape=(field((TILES, SLOT, 128)), field((...]
    pallas_call x1, Pallas kernels: 4.33 us -> 3.76 us  [shards(): pl.pallas_call(fine_kernel, out_shape=(field((2, LEV, 3, 80, 128)), shape...]
  transfers between devices with their start and end apart: 1 -> 1, of which waited for: 1 -> 1; matrix products, arithmetic and copies ran while one was open for 0% -> 0% of each run, Pallas kernels for 4% -> 5%
where the time goes in v4:
time: 55.9 us; the launch traced here: 55.2 us
  blocking collectives  33.8 us (60%)
  waiting for transfers between devices  8.83 us (16%)
  Pallas kernels  8.01 us (14%)
  starting transfers between devices  3.91 us (7%)
  between operations  0.67 us (1%)
    all_to_all x1, blocking collectives, shards(): got_tile = near(lax.all_to_all(send, 'tile', 0, 0))  18.9 us
    all_to_all x1, blocking collectives, shards(): got_grp = near(lax.all_to_all(send, 'grp', 0, 0))  14.9 us
    all_to_all x1, waiting for transfers between devices, shards(): got = lax.all_to_all(back, ('grp', 'tile'), 0, 0)  8.83 us
    all_to_all x1, starting transfers between devices, shards(): got = lax.all_to_all(back, ('grp', 'tile'), 0, 0)  3.91 us
    pallas_call x1, Pallas kernels, shards(): pl.pallas_call(fine_kernel, out_shape=(field((2, LEV, 3, 80, 128)), shape...  3.76 us
    pallas_call x1, Pallas kernels, shards(): pl.pallas_call(finish_kernel, out_shape=(shape((LEV, ROWS, COLS), f32), s...  2.5 us
    pallas_call x1, Pallas kernels, shards(): pl.pallas_call(pack_kernel, out_shape=(field((TILES, SLOT, 128)), field((...  1.74 us
  transfers between devices with their start and end apart: 1, of which 1 were waited for; matrix products, arithmetic and copies ran while one was open for 0% of the time, Pallas kernels for 5%

profile of v4, /device:TPU:1, one launch (start us, length us, event | category | flops | bytes accessed | tf_op | source)
XLA Modules:
  0.0 55.2 jit_solution(6067302601532954794)
XLA Ops:
  0.6 1.7 %pack.1 = (f32[8,136,128]{2,1,0:T(8,128)S(1)}, f32[16,128]{1,0:T(8,128)S(1)}, s32[16]{0:T(128)S(4)}, f32[4,40,320]{2,1,0:T(8,128)S(1)}) custom-call(s32[16]{0:T(128)} %rows_at.1, s32[16]{0:T(128)} %offs_at.1, s32[16]{0:T(128)} %left_at.1, s32[16]{0:T(128)} %height_at.1, s32[16]{0:T(128)} %width_at.1, f32[4,64,128]{2,1,0:T(8,128)} %so2.3, ...), custom_call_target="tpu_custom_call" | custom-call | tf_op jit(solution)/shard_map/pack/pallas_call | solution.py:461
  2.4 18.9 %all_to_all.15.got.got_tile = f32[8,136,128]{2,1,0:T(8,128)S(1)} all-to-all(f32[8,136,128]{2,1,0:T(8,128)S(1)} %get-tuple-element.12), channel_id=1, replica_groups=mesh['grp'=16,'tile'=8] {'tile'}, dimensions={0} | all-to-all | bytes 1114112 | tf_op jit(solution)/shard_map/all_to_all | solution.py:480
  21.3 14.9 %all_to_all.16.got_grp = f32[16,40,128]{2,1,0:T(8,128)S(1)} all-to-all(f32[16,40,128]{2,1,0:T(8,128)S(1)} %merge.1), channel_id=1, replica_groups=mesh['grp'=16,'tile'=8] {'grp'}, dimensions={0} | all-to-all | bytes 655360 | tf_op jit(solution)/shard_map/all_to_all | solution.py:488
  36.2 3.8 %fine.1 = (f32[2,4,3,80,128]{4,3,2,1,0:T(8,128)S(1)}, f32[128,4,128]{2,1,0:T(4,128)}) custom-call(s32[16]{0:T(128)S(4)} %get-tuple-element.11.facts, f32[8,136,128]{2,1,0:T(8,128)S(1)} %all_to_all.15.got.got_tile, f32[16,40,128]{2,1,0:T(8,128)S(1)} %all_to_all.16.got_grp, f32[4,40,320]{2,1,0:T(8,128)S(1)} %get-tuple-element.14.nx), custom_call_target="tpu_custom_call" | custom-call | tf_op jit(solution)/shard_map/fine/pallas_call | solution.py:489
  40.0 3.9 %all-to-all-start.2 = ((f32[128,4,128]{2,1,0:T(4,128)}), f32[128,4,128]{2,1,0:T(4,128)S(1)}, u32[]{:S(2)}, u32[]{:S(2)}) async-start(f32[128,4,128]{2,1,0:T(4,128)} %get-tuple-element.18), calls=%async_computation.2 | async-start | bytes 524288 | tf_op jit(solution)/shard_map/all_to_all | solution.py:527
  43.9 2.5 %finish.1 = (f32[4,64,128]{2,1,0:T(8,128)}, f32[1,4,40,320]{3,2,1,0:T(8,128)}, f32[4,40,128]{2,1,0:T(8,128)S(1)}) custom-call(s32[16]{0:T(128)S(4)} %get-tuple-element.11.facts, f32[8,136,128]{2,1,0:T(8,128)S(1)} %all_to_all.15.got.got_tile, f32[16,40,128]{2,1,0:T(8,128)S(1)} %all_to_all.16.got_grp, f32[2,4,3,80,128]{4,3,2,1,0:T(8,128)S(1)} %get-tuple-element.15.c, ...), custom_call_target="tpu_custom_call" | custom-call | tf_op jit(solution)/shard_map/finish/pallas_call | solution.py:510
  46.4 8.8 %all-to-all-done.2 = f32[128,4,128]{2,1,0:T(4,128)S(1)} async-done(((f32[128,4,128]{2,1,0:T(4,128)}), f32[128,4,128]{2,1,0:T(4,128)S(1)}, u32[]{:S(2)}, u32[]{:S(2)}) %all-to-all-start.2) | async-done | bytes 262176 | tf_op jit(solution)/shard_map/all_to_all | solution.py:527
  (2 shorter events, 0.0 us)
Async XLA Ops:
  40.0 15.3 %all-to-all-start.2 = ((f32[128,4,128]{2,1,0:T(4,128)}), f32[128,4,128]{2,1,0:T(4,128)S(1)}, u32[]{:S(2)}, u32[]{:S(2)}) async-start(f32[128,4,128]{2,1,0:T(4,128)} %get-tuple-element.18), calls=%async_computation.2 | async-start | bytes 524288 | tf_op jit(solution)/shard_map/all_to_all | solution.py:527

commit v5 on v4

--- a/solution.py
+++ b/solution.py
@@ -42,7 +42,7 @@
 
 def pack_kernel(
     rows_at, offs_at, left_at, height_at, width_at, so2, east, north, diff, nest,
-    send, edges, facts, nx,
+    send, edges, facts, nx, picks,
     rows, offs, left, height, width, x, cut, sems,
 ):
     t = lax.axis_index("tile")
@@ -60,8 +60,11 @@
         for i, f in enumerate((so2, east, north, diff))
     ]
     loads.append(pltpu.make_async_copy(nest.at[0], nx, sems.at[4]))
-    for c in loads:
-        c.start()
+    for k in (4, 0, 2, 1, 3):
+        loads[k].start()
+    for m in range(3):
+        away = lax.broadcasted_iota(jnp.int32, (128, 128), 0) + STARTS[m] - RATIO * lanes((128, 128))
+        picks[m] = jnp.where((away >= 0) & (away < RATIO), 1.0, 0.0).astype(jnp.bfloat16)
     for c in numbers:
         c.wait()
     n = nest_over(rows, g)
@@ -88,8 +91,20 @@
                 send[at, pl.ds(EDGE + 10 * (2 * l + m), 10), :] = nx[l, q, 128 * m : 128 * m + 128]
             side = 64 * (l % 2)
             send[at, pl.ds(EDGE + 80 + 10 * (l // 2), 10), side : side + 64] = nx[l, q, 256:320]
-    for c in loads[:4]:
-        c.wait()
+    loads[0].wait()
+    loads[2].wait()
+    sub = lax.broadcasted_iota(jnp.int32, (8, 128), 0)
+    ends = jnp.where(((sub == 0) & (lane == 0)) | ((sub == 1) & (lane == 127)), 1.0, 0.0)
+    planes = [x[p if p < 4 else p + 4, 0:ROWS, :] for p in range(8)]
+    sides = lax.dot_general(
+        ends,
+        jnp.concatenate(planes, axis=0),
+        (((1,), (1,)), ((), ())),
+        precision=lax.Precision.HIGHEST,
+        preferred_element_type=jnp.float32,
+    )
+    loads[1].wait()
+    loads[3].wait()
     for l in range(LEV):
         edges[l : l + 1, :] = x[l, 0:1, :]
         edges[4 + l : 5 + l, :] = x[4 + l, 0:1, :]
@@ -109,16 +124,6 @@
             jnp.where(lane < 32, part[0], part[1]),
             jnp.where(lane < 96, part[2], part[3]),
         )
-    sub = lax.broadcasted_iota(jnp.int32, (8, 128), 0)
-    ends = jnp.where(((sub == 0) & (lane == 0)) | ((sub == 1) & (lane == 127)), 1.0, 0.0)
-    planes = [x[p if p < 4 else p + 4, 0:ROWS, :] for p in range(8)]
-    sides = lax.dot_general(
-        ends,
-        jnp.concatenate(planes, axis=0),
-        (((1,), (1,)), ((), ())),
-        precision=lax.Precision.HIGHEST,
-        preferred_element_type=jnp.float32,
-    )
     for d in range(TILES):
         for l in range(5):
             send[d, 6 * l : 6 * l + 6, :] = cut[l, 4 * d : 4 * d + 6, :]
@@ -164,7 +169,7 @@
 
 
 def fine_kernel(
-    facts, got_tile, got_grp, nx,
+    facts, got_tile, got_grp, nx, picks,
     c, back,
     slot, last_part, e, raw, am, ap, bm, bp, ac, kz, sums, sems,
 ):
@@ -258,13 +263,15 @@
         wide = lanes((n, 128))
         q = slice(at, at + n)
         raw[l, 0, q, :] = parts[0]
-        raw[l, 1, q, :] = jnp.where(wide < 32, pltpu.roll(parts[0], 32, 1), pltpu.roll(parts[1], 32, 1))
-        third = pltpu.roll(parts[2], 64, 1) if turn else parts[2]
-        raw[l, 2, q, :] = jnp.where(wide < 64, pltpu.roll(parts[1], 64, 1), third)
+        raw[l, 1, q, :] = pltpu.roll(jnp.where(wide < 96, parts[1], parts[0]), 32, 1)
+        if turn:
+            raw[l, 2, q, :] = pltpu.roll(jnp.where(wide < 64, parts[2], parts[1]), 64, 1)
+        else:
+            raw[l, 2, q, :] = jnp.where(wide < 64, pltpu.roll(parts[1], 64, 1), parts[2])
 
     for l in range(LEV):
-        last_part[l, :, 64:128] = nx[l, :, 256:320]
-        lay(l, 10, OWN, (nx[l, :, 0:128], nx[l, :, 128:256], last_part[l]), False)
+        last_part[l, :, 0:64] = nx[l, :, 256:320]
+        lay(l, 10, OWN, (nx[l, :, 0:128], nx[l, :, 128:256], last_part[l]), True)
         for tile, at in ((prev_t, 0), (next_t, OWN + 10)):
             spots = (EDGE + 20 * l, EDGE + 20 * l + 10, EDGE + 80 + 10 * (l // 2))
             lay(l, at, 10, [got_tile[tile, k : k + 10, :] for k in spots], l % 2 == 0)
@@ -324,10 +331,8 @@
         value = value - high.astype(jnp.float32)
         middle = value.astype(jnp.bfloat16)
         low = (value - middle.astype(jnp.float32)).astype(jnp.bfloat16)
-        away = lax.broadcasted_iota(jnp.int32, (128, 128), 0) + STARTS[m] - RATIO * lanes((128, 128))
-        pick = jnp.where((away >= 0) & (away < RATIO), 1.0, 0.0).astype(jnp.bfloat16)
         parts = jnp.concatenate([high, middle, low], axis=0)
-        mean = mean + jnp.dot(parts, pick, preferred_element_type=jnp.float32)
+        mean = mean + jnp.dot(parts, picks[m], preferred_element_type=jnp.float32)
     mean = mean[0:16] + (mean[16:32] + mean[32:48])
     mean = mean * (1.0 / (RATIO * RATIO))
     lane4 = lanes((4, 128))
@@ -458,16 +463,17 @@
     field = functools.partial(pltpu.VMEM, dtype=f32)
     near = functools.partial(pltpu.with_memory_space_constraint, memory_space=pltpu.VMEM)
     scalar = functools.partial(pltpu.with_memory_space_constraint, memory_space=pltpu.SMEM)
-    send, edges, facts, own = pl.pallas_call(
+    send, edges, facts, own, picks = pl.pallas_call(
         pack_kernel,
         out_shape=(
             field((TILES, SLOT, 128)),
             field((16, 128)),
             pltpu.SMEM((16,), jnp.int32),
             field((LEV, OWN, WIDE)),
+            pltpu.VMEM((3, 128, 128), jnp.bfloat16),
         ),
         in_specs=[ANY] * 10,
-        out_specs=(VMEM, VMEM, SMEM, VMEM),
+        out_specs=(VMEM, VMEM, SMEM, VMEM, VMEM),
         scratch_shapes=[pltpu.SMEM((16,), jnp.int32)] * 5
         + [
             field((16, ROWS + 8, 128)),
@@ -489,7 +495,7 @@
     c, back = pl.pallas_call(
         fine_kernel,
         out_shape=(field((2, LEV, 3, 80, 128)), shape((GROUPS * TILES, 4, 128), f32)),
-        in_specs=[SMEM] + [VMEM] * 3,
+        in_specs=[SMEM] + [VMEM] * 4,
         out_specs=(VMEM, ANY),
         scratch_shapes=[
             field((4, 128)),
@@ -506,7 +512,7 @@
             dma((2,)),
         ],
         name="fine",
-    )(facts, got_tile, got_grp, near(own))
+    )(facts, got_tile, got_grp, near(own), near(picks))
     stepped, nest_next, keep = pl.pallas_call(
         finish_kernel,
         out_shape=(

time: 55.9 us -> 55.7 us (level)
  no operation moved by 1% of the time
where the time goes in v5:
time: 55.7 us; the launch traced here: 55.1 us
  blocking collectives  33.8 us (61%)
  waiting for transfers between devices  8.83 us (16%)
  Pallas kernels  7.9 us (14%)
  starting transfers between devices  3.92 us (7%)
  between operations  0.67 us (1%)
    all_to_all x1, blocking collectives, shards(): got_tile = near(lax.all_to_all(send, 'tile', 0, 0))  18.9 us
    all_to_all x1, blocking collectives, shards(): got_grp = near(lax.all_to_all(send, 'grp', 0, 0))  14.9 us
    all_to_all x1, waiting for transfers between devices, shards(): got = lax.all_to_all(back, ('grp', 'tile'), 0, 0)  8.83 us
    all_to_all x1, starting transfers between devices, shards(): got = lax.all_to_all(back, ('grp', 'tile'), 0, 0)  3.92 us
    pallas_call x1, Pallas kernels, shards(): pl.pallas_call(fine_kernel, out_shape=(field((2, LEV, 3, 80, 128)), shape...  3.68 us
    pallas_call x1, Pallas kernels, shards(): pl.pallas_call(finish_kernel, out_shape=(shape((LEV, ROWS, COLS), f32), s...  2.5 us
    pallas_call x1, Pallas kernels, shards(): pl.pallas_call(pack_kernel, out_shape=(field((TILES, SLOT, 128)), field((...  1.7 us
  transfers between devices with their start and end apart: 1, of which 1 were waited for; matrix products, arithmetic and copies ran while one was open for 0% of the time, Pallas kernels for 5%

profile of v5, /device:TPU:1, one launch (start us, length us, event | category | flops | bytes accessed | tf_op | source)
XLA Modules:
  0.0 55.1 jit_solution(11490914030367273830)
XLA Ops:
  0.6 1.7 %pack.1 = (f32[8,136,128]{2,1,0:T(8,128)S(1)}, f32[16,128]{1,0:T(8,128)S(1)}, s32[16]{0:T(128)S(4)}, f32[4,40,320]{2,1,0:T(8,128)S(1)}, bf16[3,128,128]{2,1,0:T(8,128)(2,1)S(1)}) custom-call(s32[16]{0:T(128)} %rows_at.1, s32[16]{0:T(128)} %offs_at.1, s32[16]{0:T(128)} %left_at.1, s32[16]{0:T(128)} %height_at.1, s32[16]{0:T(128)} %width_at.1, ...), custom_call_target="tpu_custom_call" | custom-call | tf_op jit(solution)/shard_map/pack/pallas_call | solution.py:466
  2.3 18.9 %all_to_all.15.got.got_tile = f32[8,136,128]{2,1,0:T(8,128)S(1)} all-to-all(f32[8,136,128]{2,1,0:T(8,128)S(1)} %get-tuple-element.13), channel_id=1, replica_groups=mesh['grp'=16,'tile'=8] {'tile'}, dimensions={0} | all-to-all | bytes 1114112 | tf_op jit(solution)/shard_map/all_to_all | solution.py:486
  21.3 14.9 %all_to_all.16.got_grp = f32[16,40,128]{2,1,0:T(8,128)S(1)} all-to-all(f32[16,40,128]{2,1,0:T(8,128)S(1)} %merge.1), channel_id=1, replica_groups=mesh['grp'=16,'tile'=8] {'grp'}, dimensions={0} | all-to-all | bytes 655360 | tf_op jit(solution)/shard_map/all_to_all | solution.py:494
  36.2 3.7 %fine.1 = (f32[2,4,3,80,128]{4,3,2,1,0:T(8,128)S(1)}, f32[128,4,128]{2,1,0:T(4,128)}) custom-call(s32[16]{0:T(128)S(4)} %get-tuple-element.12.facts, f32[8,136,128]{2,1,0:T(8,128)S(1)} %all_to_all.15.got.got_tile, f32[16,40,128]{2,1,0:T(8,128)S(1)} %all_to_all.16.got_grp, f32[4,40,320]{2,1,0:T(8,128)S(1)} %get-tuple-element.15.nx, ...), custom_call_target="tpu_custom_call" | custom-call | tf_op jit(solution)/shard_map/fine/pallas_call | solution.py:495
  39.8 3.9 %all-to-all-start.2 = ((f32[128,4,128]{2,1,0:T(4,128)}), f32[128,4,128]{2,1,0:T(4,128)S(1)}, u32[]{:S(2)}, u32[]{:S(2)}) async-start(f32[128,4,128]{2,1,0:T(4,128)} %get-tuple-element.20), calls=%async_computation.2 | async-start | bytes 524288 | tf_op jit(solution)/shard_map/all_to_all | solution.py:533
  43.8 2.5 %finish.1 = (f32[4,64,128]{2,1,0:T(8,128)}, f32[1,4,40,320]{3,2,1,0:T(8,128)}, f32[4,40,128]{2,1,0:T(8,128)S(1)}) custom-call(s32[16]{0:T(128)S(4)} %get-tuple-element.12.facts, f32[8,136,128]{2,1,0:T(8,128)S(1)} %all_to_all.15.got.got_tile, f32[16,40,128]{2,1,0:T(8,128)S(1)} %all_to_all.16.got_grp, f32[2,4,3,80,128]{4,3,2,1,0:T(8,128)S(1)} %get-tuple-element.17.c, ...), custom_call_target="tpu_custom_call" | custom-call | tf_op jit(solution)/shard_map/finish/pallas_call | solution.py:516
  46.3 8.8 %all-to-all-done.2 = f32[128,4,128]{2,1,0:T(4,128)S(1)} async-done(((f32[128,4,128]{2,1,0:T(4,128)}), f32[128,4,128]{2,1,0:T(4,128)S(1)}, u32[]{:S(2)}, u32[]{:S(2)}) %all-to-all-start.2) | async-done | bytes 262176 | tf_op jit(solution)/shard_map/all_to_all | solution.py:533
  (2 shorter events, 0.0 us)
Async XLA Ops:
  39.8 15.3 %all-to-all-start.2 = ((f32[128,4,128]{2,1,0:T(4,128)}), f32[128,4,128]{2,1,0:T(4,128)S(1)}, u32[]{:S(2)}, u32[]{:S(2)}) async-start(f32[128,4,128]{2,1,0:T(4,128)} %get-tuple-element.20), calls=%async_computation.2 | async-start | bytes 524288 | tf_op jit(solution)/shard_map/all_to_all | solution.py:533

commit v6 on v5

--- a/solution.py
+++ b/solution.py
@@ -306,17 +306,8 @@
                         value = value + flow[l] * now[l + 1]
                     c[new, l, m, r : r + 8, :] = value
 
-    def steps(count, tiles):
-        def body(_, carry):
-            advance(0, 1, tiles)
-            advance(1, 0, tiles)
-            return carry
-
-        lax.fori_loop(0, count, body, 0)
-
-    steps(2, range(8))
-    steps(2, range(7))
-    steps(1, range(1, 7))
+    for k in range(RATIO):
+        advance(k % 2, 1 - k % 2, range(0 if k < 7 else 1, 8 if k < 3 else 7))
     mean = jnp.zeros((48, 128), jnp.float32)
     wide = lanes((16, 128))
     for m in range(3):

time: 55.7 us -> 55.2 us (level); the launches traced: 55.1 us -> 55.3 us
    pallas_call x1, Pallas kernels: 0.01 us -> 0.73 us  [shards(): pl.pallas_call(place_kernel, out_shape=shape((LEV, ROWS, COLS), f32), in_...]
where the time goes in v6:
time: 55.2 us; the launch traced here: 55.3 us
  blocking collectives  33.8 us (61%)
  waiting for transfers between devices  8.83 us (16%)
  Pallas kernels  8.13 us (15%)
  starting transfers between devices  3.9 us (7%)
  between operations  0.67 us (1%)
    all_to_all x1, blocking collectives, shards(): got_tile = near(lax.all_to_all(send, 'tile', 0, 0))  18.9 us
    all_to_all x1, blocking collectives, shards(): got_grp = near(lax.all_to_all(send, 'grp', 0, 0))  14.9 us
    all_to_all x1, waiting for transfers between devices, shards(): got = lax.all_to_all(back, ('grp', 'tile'), 0, 0)  8.83 us
    all_to_all x1, starting transfers between devices, shards(): got = lax.all_to_all(back, ('grp', 'tile'), 0, 0)  3.9 us
    pallas_call x1, Pallas kernels, shards(): pl.pallas_call(fine_kernel, out_shape=(field((2, LEV, 3, 80, 128)), shape...  3.19 us
    pallas_call x1, Pallas kernels, shards(): pl.pallas_call(finish_kernel, out_shape=(shape((LEV, ROWS, COLS), f32), s...  2.5 us
    pallas_call x1, Pallas kernels, shards(): pl.pallas_call(pack_kernel, out_shape=(field((TILES, SLOT, 128)), field((...  1.7 us
  transfers between devices with their start and end apart: 1, of which 1 were waited for; matrix products, arithmetic and copies ran while one was open for 0% of the time, Pallas kernels for 5%

profile of v6, /device:TPU:1, one launch (start us, length us, event | category | flops | bytes accessed | tf_op | source)
XLA Modules:
  0.0 55.3 jit_solution(10878284669500540238)
XLA Ops:
  0.6 1.7 %pack.1 = (f32[8,136,128]{2,1,0:T(8,128)S(1)}, f32[16,128]{1,0:T(8,128)S(1)}, s32[16]{0:T(128)S(4)}, f32[4,40,320]{2,1,0:T(8,128)S(1)}, bf16[3,128,128]{2,1,0:T(8,128)(2,1)S(1)}) custom-call(s32[16]{0:T(128)} %rows_at.1, s32[16]{0:T(128)} %offs_at.1, s32[16]{0:T(128)} %left_at.1, s32[16]{0:T(128)} %height_at.1, s32[16]{0:T(128)} %width_at.1, ...), custom_call_target="tpu_custom_call" | custom-call | tf_op jit(solution)/shard_map/pack/pallas_call | solution.py:457
  2.3 18.9 %all_to_all.15.got.got_tile = f32[8,136,128]{2,1,0:T(8,128)S(1)} all-to-all(f32[8,136,128]{2,1,0:T(8,128)S(1)} %get-tuple-element.13), channel_id=1, replica_groups=mesh['grp'=16,'tile'=8] {'tile'}, dimensions={0} | all-to-all | bytes 1114112 | tf_op jit(solution)/shard_map/all_to_all | solution.py:477
  21.3 14.9 %all_to_all.16.got_grp = f32[16,40,128]{2,1,0:T(8,128)S(1)} all-to-all(f32[16,40,128]{2,1,0:T(8,128)S(1)} %merge.1), channel_id=1, replica_groups=mesh['grp'=16,'tile'=8] {'grp'}, dimensions={0} | all-to-all | bytes 655360 | tf_op jit(solution)/shard_map/all_to_all | solution.py:485
  36.2 3.2 %fine.1 = (f32[2,4,3,80,128]{4,3,2,1,0:T(8,128)S(1)}, f32[128,4,128]{2,1,0:T(4,128)}) custom-call(s32[16]{0:T(128)S(4)} %get-tuple-element.12.facts, f32[8,136,128]{2,1,0:T(8,128)S(1)} %all_to_all.15.got.got_tile, f32[16,40,128]{2,1,0:T(8,128)S(1)} %all_to_all.16.got_grp, f32[4,40,320]{2,1,0:T(8,128)S(1)} %get-tuple-element.15.nx, ...), custom_call_target="tpu_custom_call" | custom-call | tf_op jit(solution)/shard_map/fine/pallas_call | solution.py:486
  39.4 3.9 %all-to-all-start.2 = ((f32[128,4,128]{2,1,0:T(4,128)}), f32[128,4,128]{2,1,0:T(4,128)S(1)}, u32[]{:S(2)}, u32[]{:S(2)}) async-start(f32[128,4,128]{2,1,0:T(4,128)} %get-tuple-element.20), calls=%async_computation.2 | async-start | bytes 524288 | tf_op jit(solution)/shard_map/all_to_all | solution.py:524
  43.3 2.5 %finish.1 = (f32[4,64,128]{2,1,0:T(8,128)}, f32[1,4,40,320]{3,2,1,0:T(8,128)}, f32[4,40,128]{2,1,0:T(8,128)S(1)}) custom-call(s32[16]{0:T(128)S(4)} %get-tuple-element.12.facts, f32[8,136,128]{2,1,0:T(8,128)S(1)} %all_to_all.15.got.got_tile, f32[16,40,128]{2,1,0:T(8,128)S(1)} %all_to_all.16.got_grp, f32[2,4,3,80,128]{4,3,2,1,0:T(8,128)S(1)} %get-tuple-element.17.c, ...), custom_call_target="tpu_custom_call" | custom-call | tf_op jit(solution)/shard_map/finish/pallas_call | solution.py:507
  45.8 8.8 %all-to-all-done.2 = f32[128,4,128]{2,1,0:T(4,128)S(1)} async-done(((f32[128,4,128]{2,1,0:T(4,128)}), f32[128,4,128]{2,1,0:T(4,128)S(1)}, u32[]{:S(2)}, u32[]{:S(2)}) %all-to-all-start.2) | async-done | bytes 262176 | tf_op jit(solution)/shard_map/all_to_all | solution.py:524
  54.6 0.7 %place.1 = f32[4,64,128]{2,1,0:T(8,128)} custom-call(s32[16]{0:T(128)S(4)} %get-tuple-element.12.facts, f32[4,64,128]{2,1,0:T(8,128)} %get-tuple-element.18.stepped, f32[4,40,128]{2,1,0:T(8,128)S(1)} %get-tuple-element.19.keep, f32[16,32,128]{2,1,0:T(8,128)S(1)} %bitcast.1), custom_call_target="tpu_custom_call", output_to_operand_aliasing={{}: (1, {})} | custom-call | tf_op jit(solution)/shard_map/place/pallas_call | solution.py:526
  (1 shorter events, 0.0 us)
Async XLA Ops:
  39.4 15.2 %all-to-all-start.2 = ((f32[128,4,128]{2,1,0:T(4,128)}), f32[128,4,128]{2,1,0:T(4,128)S(1)}, u32[]{:S(2)}, u32[]{:S(2)}) async-start(f32[128,4,128]{2,1,0:T(4,128)} %get-tuple-element.20), calls=%async_computation.2 | async-start | bytes 524288 | tf_op jit(solution)/shard_map/all_to_all | solution.py:524
